TPU v7x, 512 devices: a whole 4x8x8 slice. The times are simulated.
512 devices in a mesh: dp: 32 (over x, z), tensor: 16 (over y, core).
Axes of the slice: x: 4, y: 8, z: 8, core: 2. Of those that a mesh axis runs over, the one named last changes fastest.
Arguments:
- tokens: bfloat16 [512, 3072], P('dp'), may hold values from -6 to 6
- cotangent: bfloat16 [512, 3072], P('dp'), may hold values from -6 to 6
- routes: int32 [512, 2], P('dp'), may hold values from 0 to 7, all different within a row; in each aligned block of 16 rows (0 to 15, 16 to 31, ...) at most 8 rows name the same one
- gates: float32 [512, 2], P('dp'), may hold values from 0.2 to 1
- w_gate: bfloat16 [3072, 131072], P(None, ('dp', 'tensor')), may hold values from -0.109375 to 0.109375
- w_up: bfloat16 [3072, 131072], P(None, ('dp', 'tensor')), may hold values from -0.109375 to 0.109375
- w_down: bfloat16 [131072, 3072], P('dp', 'tensor'), may hold values from -0.046875 to 0.046875
Outputs:
- mixed_out: bfloat16 [512, 3072], P('dp', 'tensor')
- d_tokens: bfloat16 [512, 3072], P('dp', 'tensor')
Inputs may be any that keep to these rules, and one draw needn't show every extreme that they name: `routes`: among the tokens of one index of dp (aligned blocks of 16 rows) no expert is chosen more than 8 times, and some expert is chosen exactly 8 times; the 2 experts of a token differ.
All inputs are finite; a program needn't handle non-finite values.
Results may differ from a plain program's by a relative error of at most 0.0057.
Values may be sent and summed in bfloat16 or wider, within the bound.
No kernel may reach another device: no remote copies, remote signals or barrier semaphores. Data moves between devices by JAX's collectives and lax.ppermute only.
A program may use at most 64 MiB of HBM per device.

v0:
```python
import jax
import jax.numpy as jnp
from jax import lax
from jax.sharding import PartitionSpec as P

EXPERTS = 8
CAP = 8


def dot_last(left, right):
    return lax.dot_general(
        left, right, (((1,), (1,)), ((), ())), preferred_element_type=jnp.float32
    )


def body(tokens, cotangent, routes, gates, w_gate, w_up, w_down):
    count_tok, model_width = tokens.shape
    top_k = routes.shape[1]
    n_data = lax.axis_size("dp")
    copies = n_data // EXPERTS
    slot_count = EXPERTS * CAP
    flat_routes = routes.reshape(-1)
    onehot = (flat_routes[:, None] == jnp.arange(EXPERTS, dtype=jnp.int32)[None, :]).astype(
        jnp.int32
    )
    before = jnp.cumsum(onehot, axis=0) - onehot
    target = flat_routes * CAP + jnp.sum(before * onehot, axis=1)
    placing = jnp.arange(slot_count, dtype=jnp.int32)[:, None] == target[None, :]
    place_half = placing.astype(jnp.bfloat16)
    place_full = placing.astype(jnp.float32)
    x_rows = jnp.repeat(tokens, top_k, axis=0)
    dy_rows = (
        jnp.repeat(cotangent.astype(jnp.float32), top_k, axis=0) * gates.reshape(-1)[:, None]
    ).astype(jnp.bfloat16)

    def outbox(rows):
        packed = jnp.dot(place_half, rows, preferred_element_type=jnp.float32).astype(jnp.bfloat16)
        packed = packed.reshape(EXPERTS, CAP, rows.shape[1])
        return jnp.repeat(packed, copies, axis=0)

    got_x, got_dy = (
        lax.all_to_all(outbox(x_rows), "dp", split_axis=0, concat_axis=0, tiled=True),
        lax.all_to_all(outbox(dy_rows), "dp", split_axis=0, concat_axis=0, tiled=True),
    )
    rows_in = got_x.shape[0] * got_x.shape[1]
    x_in = got_x.reshape(rows_in, model_width)
    dy_in = got_dy.reshape(rows_in, model_width)
    gate_pre = jnp.dot(x_in, w_gate, preferred_element_type=jnp.float32)
    up_pre = jnp.dot(x_in, w_up, preferred_element_type=jnp.float32)
    sigmoid_gate = jax.nn.sigmoid(gate_pre)
    activated = gate_pre * sigmoid_gate
    hidden = (activated * up_pre).astype(jnp.bfloat16)
    col_width = w_down.shape[1]
    out_part = jnp.dot(
        lax.all_gather(hidden, "tensor", axis=1, tiled=True),
        w_down,
        preferred_element_type=jnp.float32,
    )
    gate_turned, up_turned, down_turned = (
        lax.all_to_all(w_gate, "tensor", split_axis=0, concat_axis=1, tiled=True),
        lax.all_to_all(w_up, "tensor", split_axis=0, concat_axis=1, tiled=True),
        lax.all_to_all(w_down, "tensor", split_axis=0, concat_axis=1, tiled=True),
    )
    d_hidden = dot_last(dy_in, down_turned)
    d_gate = (d_hidden * up_pre * sigmoid_gate * (1.0 + gate_pre * (1.0 - sigmoid_gate))).astype(
        jnp.bfloat16
    )
    d_up = (d_hidden * activated).astype(jnp.bfloat16)
    grad_part = dot_last(
        lax.all_gather(d_gate, "tensor", axis=1, tiled=True), gate_turned
    ) + dot_last(lax.all_gather(d_up, "tensor", axis=1, tiled=True), up_turned)
    back_out, back_grad = (
        lax.all_to_all(
            out_part.reshape(n_data, CAP, col_width), "dp", split_axis=0, concat_axis=0, tiled=True
        ),
        lax.all_to_all(
            grad_part.reshape(n_data, CAP, col_width), "dp", split_axis=0, concat_axis=0, tiled=True
        ),
    )

    def unpack(returned):
        summed = jnp.sum(returned.reshape(EXPERTS, copies, CAP, col_width), axis=1).reshape(
            slot_count, col_width
        )
        picked = lax.dot_general(
            place_full,
            summed,
            (((0,), (0,)), ((), ())),
            precision=lax.Precision.HIGHEST,
            preferred_element_type=jnp.float32,
        )
        return picked.reshape(count_tok, top_k, col_width)

    mixed_out = jnp.sum(unpack(back_out) * gates[:, :, None], axis=1).astype(jnp.bfloat16)
    d_tokens = jnp.sum(unpack(back_grad), axis=1).astype(jnp.bfloat16)
    return (mixed_out, d_tokens)


def solution(mesh):
    placed = (
        P("dp", None),
        P("dp", None),
        P("dp", None),
        P("dp", None),
        P(None, ("dp", "tensor")),
        P(None, ("dp", "tensor")),
        P("dp", "tensor"),
    )
    return jax.shard_map(
        body,
        mesh=mesh,
        in_specs=placed,
        out_specs=(P("dp", "tensor"), P("dp", "tensor")),
        check_vma=False,
    )
```

profile of v0, /device:TPU:8, one launch (start us, length us, event | category | flops | bytes accessed | tf_op | source)
XLA Modules:
  0.0 352.8 jit_solution(13465686441488400917)
XLA Ops:
  7.2 2.7 copy.46
  9.9 9.5 %all-to-all-start.3 = ((bf16[16,256,192]{1,2,0:T(8,128)(2,1)}), bf16[16,256,192]{1,2,0:T(8,128)(2,1)S(1)}, u32[]{:S(2)}, u32[]{:S(2)}) async-start(bf16[16,256,192]{1,2,0:T(8,128)(2,1)} %bitcast.57), calls=%async_computation.3 | async-start | bytes 3145728 | tf_op jit(solution)/shard_map/all_to_all | solution.py:62
  20.3 35.1 %all-to-all-done.3 = bf16[16,256,192]{1,2,0:T(8,128)(2,1)S(1)} async-done(((bf16[16,256,192]{1,2,0:T(8,128)(2,1)}), bf16[16,256,192]{1,2,0:T(8,128)(2,1)S(1)}, u32[]{:S(2)}, u32[]{:S(2)}) %all-to-all-start.3) | async-done | bytes 1572896 | tf_op jit(solution)/shard_map/all_to_all | solution.py:62
  55.4 1.5 broadcast_in_dim.17
  57.0 11.4 %all-to-all-start = ((bf16[32,8,3072]{2,1,0:T(8,128)(2,1)}), bf16[32,8,3072]{2,1,0:T(8,128)(2,1)S(1)}, u32[]{:S(2)}, u32[]{:S(2)}) async-start(bf16[32,8,3072]{2,1,0:T(8,128)(2,1)} %bitcast.1), calls=%async_computation | async-start | bytes 3145728 | tf_op jit(solution)/shard_map/all_to_all | solution.py:42
  68.6 0.3 reshape.117
  69.0 0.3 fusion.1
  69.4 38.8 %all-to-all-done = bf16[32,8,3072]{2,1,0:T(8,128)(2,1)S(1)} async-done(((bf16[32,8,3072]{2,1,0:T(8,128)(2,1)}), bf16[32,8,3072]{2,1,0:T(8,128)(2,1)S(1)}, u32[]{:S(2)}, u32[]{:S(2)}) %all-to-all-start) | async-done | bytes 1572896 | tf_op jit(solution)/shard_map/all_to_all | solution.py:42
  108.1 1.3 broadcast_in_dim.19
  109.5 5.8 %all-to-all-start.2 = ((bf16[32,8,3072]{2,1,0:T(8,128)(2,1)}), bf16[32,8,3072]{2,1,0:T(8,128)(2,1)}, u32[]{:S(2)}, u32[]{:S(2)}) async-start(bf16[32,8,3072]{2,1,0:T(8,128)(2,1)} %bitcast.8), calls=%async_computation.2 | async-start | bytes 3145728 | tf_op jit(solution)/shard_map/all_to_all | solution.py:43
  115.4 2.1 fusion.6
  117.5 1.3 fusion.4
  118.8 35.8 %all-to-all-done.2 = bf16[32,8,3072]{2,1,0:T(8,128)(2,1)} async-done(((bf16[32,8,3072]{2,1,0:T(8,128)(2,1)}), bf16[32,8,3072]{2,1,0:T(8,128)(2,1)}, u32[]{:S(2)}, u32[]{:S(2)}) %all-to-all-start.2) | async-done | bytes 1572896 | tf_op jit(solution)/shard_map/all_to_all | solution.py:43
  154.6 3.2 multiply_convert_fusion.1
  157.9 0.7 all-gather.6.cloned.1.call-update
  158.6 7.0 %all-to-all-start.4 = ((bf16[16,192,256]{2,1,0:T(8,128)(2,1)}), bf16[16,192,256]{2,1,0:T(8,128)(2,1)S(1)}, u32[]{:S(2)}, u32[]{:S(2)}) async-start(bf16[16,192,256]{2,1,0:T(8,128)(2,1)} %bitcast.12), calls=%async_computation.4 | async-start | bytes 3145728 | tf_op jit(solution)/shard_map/all_to_all | solution.py:60
  165.6 0.7 all-gather.8.cloned.1.call-update
  166.3 40.9 %all-to-all-done.4 = bf16[16,192,256]{2,1,0:T(8,128)(2,1)S(1)} async-done(((bf16[16,192,256]{2,1,0:T(8,128)(2,1)}), bf16[16,192,256]{2,1,0:T(8,128)(2,1)S(1)}, u32[]{:S(2)}, u32[]{:S(2)}) %all-to-all-start.4) | async-done | bytes 1572896 | tf_op jit(solution)/shard_map/all_to_all | solution.py:60
  207.2 8.1 %all-to-all-start.5 = ((bf16[16,192,256]{2,1,0:T(8,128)(2,1)}), bf16[16,192,256]{2,1,0:T(8,128)(2,1)S(1)}, u32[]{:S(2)}, u32[]{:S(2)}) async-start(bf16[16,192,256]{2,1,0:T(8,128)(2,1)} %bitcast.60), calls=%async_computation.5 | async-start | bytes 3145728 | tf_op jit(solution)/shard_map/all_to_all | solution.py:61
  215.3 1.3 copy.39
  216.6 36.5 %all-to-all-done.5 = bf16[16,192,256]{2,1,0:T(8,128)(2,1)S(1)} async-done(((bf16[16,192,256]{2,1,0:T(8,128)(2,1)}), bf16[16,192,256]{2,1,0:T(8,128)(2,1)S(1)}, u32[]{:S(2)}, u32[]{:S(2)}) %all-to-all-start.5) | async-done | bytes 1572896 | tf_op jit(solution)/shard_map/all_to_all | solution.py:61
  253.4 3.6 %convolution_bitcast_fusion = f32[32,8,192]{2,1,0:T(8,128)} fusion(bf16[256,4096]{1,0:T(8,128)(2,1)} %all-gather.4.cloned.1.call-done, bf16[4096,192]{0,1:T(8,128)(2,1)} %param.13), kind=kOutput, calls=%fused_computation.11 | convolution fusion | flops 402653184 | bytes 3866624 | tf_op jit(solution)/shard_map/dot_general | solution.py:54
  257.0 6.0 %all-to-all-start.1 = ((f32[32,8,192]{2,1,0:T(8,128)}), f32[32,8,192]{2,1,0:T(8,128)S(1)}, u32[]{:S(2)}, u32[]{:S(2)}) async-start(f32[32,8,192]{2,1,0:T(8,128)} %convolution_bitcast_fusion), calls=%async_computation.1 | async-start | bytes 524288 | tf_op jit(solution)/shard_map/all_to_all | solution.py:73
  263.0 14.1 %all-gather.6.cloned.1.call-done = bf16[256,4096]{1,0:T(8,128)(2,1)} async-done(((bf16[256,256]{1,0:T(8,128)(2,1)}), bf16[256,4096]{1,0:T(8,128)(2,1)}) %all-gather.6.cloned.1.call-update) | async-done | bytes 2097168 | tf_op jit(solution)/shard_map/all_gather | solution.py:70
  277.0 3.1 fusion.18
  280.1 39.1 %all-gather.8.cloned.1.call-done = bf16[256,4096]{1,0:T(8,128)(2,1)} async-done(((bf16[256,256]{1,0:T(8,128)(2,1)}), bf16[256,4096]{1,0:T(8,128)(2,1)}) %all-gather.8.cloned.1.call-update) | async-done | bytes 2097168 | tf_op jit(solution)/shard_map/all_gather | solution.py:71
  319.3 2.4 convolution_add_fusion
  321.7 0.8 copy.35
  322.5 10.2 %all-to-all-start.6 = ((f32[32,8,192]{2,1,0:T(8,128)}), f32[32,8,192]{2,1,0:T(8,128)S(1)}, u32[]{:S(2)}, u32[]{:S(2)}) async-start(f32[32,8,192]{2,1,0:T(8,128)} %bitcast.16), calls=%async_computation.6 | async-start | bytes 524288 | tf_op jit(solution)/shard_map/all_to_all | solution.py:76
  332.8 0.7 fusion.8
  333.6 11.9 %all-to-all-done.6 = f32[32,8,192]{2,1,0:T(8,128)S(1)} async-done(((f32[32,8,192]{2,1,0:T(8,128)}), f32[32,8,192]{2,1,0:T(8,128)S(1)}, u32[]{:S(2)}, u32[]{:S(2)}) %all-to-all-start.6) | async-done | bytes 196640 | tf_op jit(solution)/shard_map/all_to_all | solution.py:76
  345.5 0.7 convolution_reduce_fusion
  (37 shorter events, 1.8 us)
Async XLA Ops:
  9.9 9.5 %copy-start.3 = (bf16[16,3072]{1,0:T(8,128)(2,1)S(1)}, bf16[16,3072]{1,0:T(8,128)(2,1)}, u32[]{:S(2)}) copy-start(bf16[16,3072]{1,0:T(8,128)(2,1)} %param.7) | copy-start | bytes 294916
  9.9 9.7 %copy-start.6 = (s32[16,2]{0,1:T(2,128)S(1)}, s32[16,2]{0,1:T(2,128)}, u32[]{:S(2)}) copy-start(s32[16,2]{0,1:T(2,128)} %param.9) | copy-start | bytes 388
  9.9 45.5 %all-to-all-start.3 = ((bf16[16,256,192]{1,2,0:T(8,128)(2,1)}), bf16[16,256,192]{1,2,0:T(8,128)(2,1)S(1)}, u32[]{:S(2)}, u32[]{:S(2)}) async-start(bf16[16,256,192]{1,2,0:T(8,128)(2,1)} %bitcast.57), calls=%async_computation.3 | async-start | bytes 3145728 | tf_op jit(solution)/shard_map/all_to_all | solution.py:62
  55.4 1.6 copy-start.2
  56.9 11.6 %copy-start.4 = (bf16[16,3072]{1,0:T(8,128)(2,1)S(1)}, bf16[16,3072]{1,0:T(8,128)(2,1)}, u32[]{:S(2)}) copy-start(bf16[16,3072]{1,0:T(8,128)(2,1)} %param.8) | copy-start | bytes 294916
  56.9 12.0 %copy-start.5 = (f32[16,2]{0,1:T(2,128)S(1)}, f32[16,2]{0,1:T(2,128)}, u32[]{:S(2)}) copy-start(f32[16,2]{0,1:T(2,128)} %param.10) | copy-start | bytes 388
  57.0 51.1 %all-to-all-start = ((bf16[32,8,3072]{2,1,0:T(8,128)(2,1)}), bf16[32,8,3072]{2,1,0:T(8,128)(2,1)S(1)}, u32[]{:S(2)}, u32[]{:S(2)}) async-start(bf16[32,8,3072]{2,1,0:T(8,128)(2,1)} %bitcast.1), calls=%async_computation | async-start | bytes 3145728 | tf_op jit(solution)/shard_map/all_to_all | solution.py:42
  109.5 45.1 %all-to-all-start.2 = ((bf16[32,8,3072]{2,1,0:T(8,128)(2,1)}), bf16[32,8,3072]{2,1,0:T(8,128)(2,1)}, u32[]{:S(2)}, u32[]{:S(2)}) async-start(bf16[32,8,3072]{2,1,0:T(8,128)(2,1)} %bitcast.8), calls=%async_computation.2 | async-start | bytes 3145728 | tf_op jit(solution)/shard_map/all_to_all | solution.py:43
  115.3 2.2 copy-start
  115.3 138.0 %all-gather.4.cloned.1.call-start = ((), (), s32[]{:S(2)}) async-start(), calls=%async_computation.7 | async-start | bytes 2228224 | tf_op jit(solution)/shard_map/all_gather | solution.py:55
  157.8 119.2 %all-gather.6.cloned.1.call-start = ((), (), s32[]{:S(2)}) async-start(), calls=%async_computation.8 | async-start | bytes 2228224 | tf_op jit(solution)/shard_map/all_gather | solution.py:70
  158.6 48.6 %all-to-all-start.4 = ((bf16[16,192,256]{2,1,0:T(8,128)(2,1)}), bf16[16,192,256]{2,1,0:T(8,128)(2,1)S(1)}, u32[]{:S(2)}, u32[]{:S(2)}) async-start(bf16[16,192,256]{2,1,0:T(8,128)(2,1)} %bitcast.12), calls=%async_computation.4 | async-start | bytes 3145728 | tf_op jit(solution)/shard_map/all_to_all | solution.py:60
  165.6 153.7 %all-gather.8.cloned.1.call-start = ((), (), s32[]{:S(2)}) async-start(), calls=%async_computation.9 | async-start | bytes 2228224 | tf_op jit(solution)/shard_map/all_gather | solution.py:71
  207.2 46.0 %all-to-all-start.5 = ((bf16[16,192,256]{2,1,0:T(8,128)(2,1)}), bf16[16,192,256]{2,1,0:T(8,128)(2,1)S(1)}, u32[]{:S(2)}, u32[]{:S(2)}) async-start(bf16[16,192,256]{2,1,0:T(8,128)(2,1)} %bitcast.60), calls=%async_computation.5 | async-start | bytes 3145728 | tf_op jit(solution)/shard_map/all_to_all | solution.py:61
  253.3 23.7 %copy-start.1 = (bf16[16,24,8,256]{3,2,0,1:T(8,128)(2,1)S(1)}, bf16[16,24,8,256]{3,2,0,1:T(8,128)(2,1)}, u32[]{:S(2)}) copy-start(bf16[16,24,8,256]{3,2,0,1:T(8,128)(2,1)} %copy.39) | copy-start | bytes 4718596
  257.0 65.6 %all-to-all-start.1 = ((f32[32,8,192]{2,1,0:T(8,128)}), f32[32,8,192]{2,1,0:T(8,128)S(1)}, u32[]{:S(2)}, u32[]{:S(2)}) async-start(f32[32,8,192]{2,1,0:T(8,128)} %convolution_bitcast_fusion), calls=%async_computation.1 | async-start | bytes 524288 | tf_op jit(solution)/shard_map/all_to_all | solution.py:73
  322.5 23.0 %all-to-all-start.6 = ((f32[32,8,192]{2,1,0:T(8,128)}), f32[32,8,192]{2,1,0:T(8,128)S(1)}, u32[]{:S(2)}, u32[]{:S(2)}) async-start(f32[32,8,192]{2,1,0:T(8,128)} %bitcast.16), calls=%async_computation.6 | async-start | bytes 524288 | tf_op jit(solution)/shard_map/all_to_all | solution.py:76
Sparse Core Ops, SparseCore 0:
  158.0 62.6 all-gather.3
  222.7 54.3 all-gather.5
  279.1 40.1 all-gather.7
where the time goes:
time: 354 us; the launch traced here: 353 us
  waiting for transfers between devices  254 us (72%)
  starting transfers between devices  58.1 us (16%)
  matrix products  17.8 us (5%)
  between operations  13.9 us (4%)
  local copies, waits for them, and re-layouts  8.97 us (3%)
    all_to_all x1, waiting for transfers between devices, body(): lax.all_to_all(w_gate, 'tensor', split_axis=0, concat_axis=1, tiled=True)  40.9 us
    all_gather x1, waiting for transfers between devices, body(): lax.all_gather(d_up, 'tensor', axis=1, tiled=True)  39.1 us
    all_to_all x1, waiting for transfers between devices, body(): lax.all_to_all(outbox(x_rows), 'dp', split_axis=0, concat_axis=0, tiled=T...  38.8 us
    all_to_all x1, waiting for transfers between devices, body(): lax.all_to_all(w_up, 'tensor', split_axis=0, concat_axis=1, tiled=True)  36.5 us
    all_to_all x1, waiting for transfers between devices, body(): lax.all_to_all(outbox(dy_rows), 'dp', split_axis=0, concat_axis=0, tiled=...  35.8 us
    all_to_all x1, waiting for transfers between devices, body(): lax.all_to_all(w_down, 'tensor', split_axis=0, concat_axis=1, tiled=True)  35.1 us
    all_gather x1, waiting for transfers between devices, body(): lax.all_gather(d_gate, 'tensor', axis=1, tiled=True)  14.1 us
    all_to_all x1, waiting for transfers between devices, body(): lax.all_to_all(grad_part.reshape(n_data, CAP, col_width), 'dp', split_axi...  11.9 us
  transfers between devices with their start and end apart: 10, of which 8 were waited for; matrix products, arithmetic and copies ran while one was open for 5% of the time, Pallas kernels for 0%

commit v1 on v0

v1 whole, which is shorter than its diff:
```python
import jax
import jax.numpy as jnp
from jax import lax
from jax.sharding import Mesh, PartitionSpec as P

EXPERTS = 8
CAP = 8
DP = ("x", "z")
SWAP = ((0, 1), (1, 0))


def mm(a, b):
    return jnp.dot(a, b, preferred_element_type=jnp.float32)


def mm_t(a, b):
    return lax.dot_general(a, b, (((1,), (1,)), ((), ())), preferred_element_type=jnp.float32)


def turn_down(w_down, core, row, rows):
    cols = w_down.shape[1]
    width = w_down.shape[0] // (2 * rows)
    down = w_down.T.reshape(cols, rows, 2, width)
    own = lax.dynamic_index_in_dim(down, core, 2, keepdims=False).transpose(1, 0, 2)
    away = lax.dynamic_index_in_dim(down, 1 - core, 2, keepdims=False).transpose(1, 0, 2)
    other = lax.ppermute(away, "c", SWAP)
    both = jnp.stack([own, other], axis=1)
    got = both
    for shift in (1, 7, 2, 6, 3, 5, 4):
        perm = [(i, (i + shift) % rows) for i in range(rows)]
        piece = lax.dynamic_index_in_dim(both, (row + shift) % rows, 0, keepdims=False)
        piece = lax.ppermute(piece, "y", perm)
        got = lax.dynamic_update_index_in_dim(got, piece, (row - shift) % rows, 0)
    return got[:, 0].reshape(rows * cols, width), got[:, 1].reshape(rows * cols, width)


def body(tokens, cotangent, routes, gates, w_gate, w_up, w_down):
    count_tok, model = tokens.shape
    top = routes.shape[1]
    half = model // 2
    n_dp = lax.axis_size(DP)
    rows = lax.axis_size("y")
    copies = n_dp // EXPERTS
    slots = EXPERTS * CAP
    core, row = lax.axis_index("c"), lax.axis_index("y")
    cols = w_down.shape[1]

    down_own, down_other = turn_down(w_down, core, row, rows)

    flat = routes.reshape(-1)
    order = jnp.arange(flat.shape[0], dtype=jnp.int32)
    earlier = (flat[:, None] == flat[None, :]) & (order[None, :] < order[:, None])
    target = flat * CAP + jnp.sum(earlier.astype(jnp.int32), axis=1)
    placing = jnp.arange(slots, dtype=jnp.int32)[:, None] == target[None, :]
    slot_gate = jnp.sum(jnp.where(placing, gates.reshape(-1)[None, :], 0.0), axis=1)
    of_token = jnp.any(placing.reshape(slots, count_tok, top), axis=2).astype(jnp.bfloat16)
    x_half = lax.dynamic_slice_in_dim(tokens, core * half, half, 1)
    dy_half = lax.dynamic_index_in_dim(
        cotangent.reshape(count_tok, rows, 2, cols), core, 2, keepdims=False
    ).reshape(count_tok, half)
    x_out = mm(of_token, x_half).astype(jnp.bfloat16)
    dy_out = (mm(of_token, dy_half) * slot_gate[:, None]).astype(jnp.bfloat16)
    packed = jnp.concatenate([x_out, dy_out], axis=1).reshape(EXPERTS, CAP, model)
    sent = jnp.repeat(packed, copies, axis=0)
    got = lax.all_to_all(sent, DP, split_axis=0, concat_axis=0, tiled=True)
    got = got.reshape(n_dp * CAP, model)
    partner = lax.ppermute(got, "c", SWAP)
    x_low = jnp.where(core == 0, got[:, :half], partner[:, :half])
    x_high = jnp.where(core == 0, partner[:, :half], got[:, :half])
    x_in = jnp.concatenate([x_low, x_high], axis=1)

    gate_pre = mm(x_in, w_gate)
    up_pre = mm(x_in, w_up)
    s = jax.nn.sigmoid(gate_pre)
    activated = gate_pre * s
    hidden = (activated * up_pre).astype(jnp.bfloat16)
    d_hidden = mm(got[:, half:], down_own) + mm(partner[:, half:], down_other)
    d_gate = (d_hidden * up_pre * s * (1.0 + gate_pre * (1.0 - s))).astype(jnp.bfloat16)
    d_up = (d_hidden * activated).astype(jnp.bfloat16)

    gate_rows = w_gate.reshape(rows, 2, cols, -1)
    up_rows = w_up.reshape(rows, 2, cols, -1)

    def partial(parity, down):
        g = lax.dynamic_index_in_dim(gate_rows, parity, 1, keepdims=False).reshape(half, -1)
        u = lax.dynamic_index_in_dim(up_rows, parity, 1, keepdims=False).reshape(half, -1)
        out = mm_t(hidden, down).reshape(-1, rows, cols)
        grad = (mm_t(d_gate, g) + mm_t(d_up, u)).reshape(-1, rows, cols)
        return jnp.concatenate([out, grad], axis=2).transpose(1, 0, 2)

    away = partial(1 - core, down_other).astype(jnp.bfloat16)
    near = partial(core, down_own)
    total = (near + lax.ppermute(away, "c", SWAP).astype(jnp.float32)).astype(jnp.bfloat16)
    back = lax.all_to_all(total, "y", split_axis=0, concat_axis=0, tiled=True)
    back = jnp.sum(back.astype(jnp.float32), axis=0).astype(jnp.bfloat16)
    back = back.reshape(n_dp, CAP, 2 * cols)
    back = lax.all_to_all(back, DP, split_axis=0, concat_axis=0, tiled=True)
    back = back.reshape(EXPERTS, copies, CAP, 2 * cols).astype(jnp.float32)
    summed = jnp.sum(back, axis=1).reshape(slots, 2 * cols)

    def unpack(weights, values):
        return lax.dot_general(
            weights,
            values,
            (((0,), (0,)), ((), ())),
            precision=lax.Precision.HIGHEST,
            preferred_element_type=jnp.float32,
        ).astype(jnp.bfloat16)

    weight = jnp.sum(
        jnp.where(placing, gates.reshape(-1)[None, :], 0.0).reshape(slots, count_tok, top), axis=2
    )
    return (
        unpack(weight, summed[:, :cols]),
        unpack(of_token.astype(jnp.float32), summed[:, cols:]),
    )


def solution(mesh):
    size = dict(x=4, z=8, y=8, c=2)
    fine = Mesh(mesh.devices.reshape(tuple(size.values())), tuple(size))
    dp, tensor = DP, ("y", "c")
    placed = (P(dp, None),) * 4 + (P(None, dp + tensor),) * 2 + (P(dp, tensor),)
    return jax.shard_map(
        body,
        mesh=fine,
        in_specs=placed,
        out_specs=(P(dp, tensor), P(dp, tensor)),
        check_vma=False,
    )
```

time: 354 us -> 186 us (0.53)
  the two profiles are of different devices: /device:TPU:8 before, /device:TPU:2 now
where the time goes in v1:
time: 186 us; the launch traced here: 185 us
  starting transfers between devices  57.7 us (31%)
  blocking collectives  44.5 us (24%)
  waiting for transfers between devices  38.5 us (21%)
  local copies, waits for them, and re-layouts  24.5 us (13%)
  matrix products  9.53 us (5%)
  other arithmetic  8.82 us (5%)
    all_to_all x1, blocking collectives, body(): back = lax.all_to_all(total, 'y', split_axis=0, concat_axis=0, tiled=True)  44.5 us
    ppermute x7, waiting for transfers between devices, turn_down(): piece = lax.ppermute(piece, 'y', perm)  28.2 us
    ppermute x7, starting transfers between devices, turn_down(): piece = lax.ppermute(piece, 'y', perm)  28.2 us
    all_to_all x1, starting transfers between devices, body(): got = lax.all_to_all(sent, DP, split_axis=0, concat_axis=0, tiled=True)  13.6 us
    all_to_all x1, waiting for transfers between devices, body(): back = lax.all_to_all(back, DP, split_axis=0, concat_axis=0, tiled=True)  10.3 us
    all_to_all x1, starting transfers between devices, body(): back = lax.all_to_all(back, DP, split_axis=0, concat_axis=0, tiled=True)  9.79 us
    unnamed x28, local copies, waits for them, and re-layouts  5.15 us
    dot_general x6, matrix products, mm_t(): lax.dot_general(a, b, (((1,), (1,)), ((), ())), preferred_element_type=jn...  4.43 us
  transfers between devices with their start and end apart: 12, of which 4 were waited for; matrix products, arithmetic and copies ran while one was open for 11% of the time, Pallas kernels for 0%

profile of v1, /device:TPU:2, one launch (start us, length us, event | category | flops | bytes accessed | tf_op | source)
XLA Modules:
  0.0 185.0 jit_solution(2256853045346137213)
XLA Ops:
  3.5 1.1 reshape.104
  5.8 1.3 broadcast_in_dim.57
  7.1 13.6 %all-to-all-start = ((bf16[32,8,3072]{2,1,0:T(8,128)(2,1)}), bf16[32,8,3072]{2,1,0:T(8,128)(2,1)}, u32[]{:S(2)}, u32[]{:S(2)}) async-start(bf16[32,8,3072]{2,1,0:T(8,128)(2,1)} %bitcast.1), calls=%async_computation | async-start | bytes 3145728 | tf_op jit(solution)/shard_map/all_to_all | solution.py:65
  20.8 1.2 reshape.109
  22.0 4.4 %constant_dynamic-slice_fusion.5 = (bf16[192,8,1,256]{3,2,1,0:T(2,128)(2,1)}, bf16[192,8,1,256]{3,2,1,0:T(2,128)(2,1)S(1)}) fusion(bf16[192,8,2,256]{3,2,1,0:T(2,128)(2,1)S(1)} %reshape.109, s32[]{:T(128)S(6)} %select_n.143, s32[]{:T(128)S(6)} %select_n.147), kind=kLoop, calls=%fused_computation.88 | loop fusion | bytes 3145736 | tf_op jit(solution)/shard_map/jit(dynamic_index_in_dim)/dynamic_slice | solution.py:24
  26.4 1.3 copy.74
  27.7 1.9 %collective-permute-start.1 = (bf16[8,192,256]{2,1,0:T(8,128)(2,1)}, bf16[8,192,256]{2,1,0:T(8,128)(2,1)S(1)}, u32[]{:S(2)}, u32[]{:S(2)}) collective-permute-start(bf16[8,192,256]{2,1,0:T(8,128)(2,1)} %bitcast.94), channel_id=1, source_target_pairs={{0,1},{1,0},{2,3},{3,2},{4,5},{5,4},{6,7},{7,6},{8,9},{9,8},{10,11... | collective-permute-start | bytes 2359304 | tf_op jit(solution)/shard_map/ppermute | solution.py:26
  30.4 3.6 %constant_dynamic-slice_fusion = (bf16[8,1,192,256]{3,2,1,0:T(8,128)(2,1)}, bf16[8,1,192,256]{3,2,1,0:T(8,128)(2,1)}, bf16[8,1,192,256]{3,2,1,0:T(8,128)(2,1)}, bf16[8,1,192,256]{3,2,1,0:T(8,128)(2,1)}) fusion(bf16[8,2,192,256]{3,2,1,0:T(8,128)(2,1)} %bitcast.111, s32[]{:T(128)S(6)} %select_n.147, s32[]{:T(128)S(6)} %select_n.143, ...), kind=kLoop, calls=%fused_computation.83 | loop fusion | bytes 6291464 | tf_op jit(solution)/shard_map/jit(dynamic_index_in_dim)/dynamic_slice | solution.py:86
  34.9 3.5 %collective-permute-start.2 = (bf16[2,192,256]{2,1,0:T(8,128)(2,1)S(1)}, bf16[2,192,256]{2,1,0:T(8,128)(2,1)S(1)}, u32[]{:S(2)}, u32[]{:S(2)}) collective-permute-start(bf16[2,192,256]{2,1,0:T(8,128)(2,1)S(1)} %get-tuple-element.11), channel_id=1, source_target_pairs={{0,2},{2,4},{4,6},{6,8},{8,10},{10,12},{12,14},{14,0},{1,3},{3,5},... | collective-permute-start | bytes 589832 | tf_op jit(solution)/shard_map/ppermute | solution.py:32
  39.1 6.0 %collective-permute-start.7 = (bf16[2,192,256]{2,1,0:T(8,128)(2,1)}, bf16[2,192,256]{2,1,0:T(8,128)(2,1)}, u32[]{:S(2)}, u32[]{:S(2)}) collective-permute-start(bf16[2,192,256]{2,1,0:T(8,128)(2,1)} %fusion.21), channel_id=1, source_target_pairs={{0,10},{2,12},{4,14},{6,0},{8,2},{10,4},{12,6},{14,8},{1,11},{3,13... | collective-permute-start | bytes 589832 | tf_op jit(solution)/shard_map/ppermute | solution.py:32
  45.1 3.8 %collective-permute-start.8 = (bf16[2,192,256]{2,1,0:T(8,128)(2,1)S(1)}, bf16[2,192,256]{2,1,0:T(8,128)(2,1)}, u32[]{:S(2)}, u32[]{:S(2)}) collective-permute-start(bf16[2,192,256]{2,1,0:T(8,128)(2,1)S(1)} %get-tuple-element.10), channel_id=1, source_target_pairs={{0,8},{2,10},{4,12},{6,14},{8,0},{10,2},{12,4},{14,6},{1,9},{3,11}... | collective-permute-start | bytes 589832 | tf_op jit(solution)/shard_map/ppermute | solution.py:32
  48.9 3.4 %collective-permute-start.3 = (bf16[2,192,256]{2,1,0:T(8,128)(2,1)S(1)}, bf16[2,192,256]{2,1,0:T(8,128)(2,1)}, u32[]{:S(2)}, u32[]{:S(2)}) collective-permute-start(bf16[2,192,256]{2,1,0:T(8,128)(2,1)S(1)} %get-tuple-element.12), channel_id=1, source_target_pairs={{0,14},{2,0},{4,2},{6,4},{8,6},{10,8},{12,10},{14,12},{1,15},{3,1}... | collective-permute-start | bytes 589832 | tf_op jit(solution)/shard_map/ppermute | solution.py:32
  52.3 4.3 %collective-permute-start.4 = (bf16[2,192,256]{2,1,0:T(8,128)(2,1)}, bf16[2,192,256]{2,1,0:T(8,128)(2,1)}, u32[]{:S(2)}, u32[]{:S(2)}) collective-permute-start(bf16[2,192,256]{2,1,0:T(8,128)(2,1)} %get-tuple-element.13), channel_id=1, source_target_pairs={{0,4},{2,6},{4,8},{6,10},{8,12},{10,14},{12,0},{14,2},{1,5},{3,7},... | collective-permute-start | bytes 589832 | tf_op jit(solution)/shard_map/ppermute | solution.py:32
  56.8 3.7 %collective-permute-start.5 = (bf16[2,192,256]{2,1,0:T(8,128)(2,1)}, bf16[2,192,256]{2,1,0:T(8,128)(2,1)S(1)}, u32[]{:S(2)}, u32[]{:S(2)}) collective-permute-start(bf16[2,192,256]{2,1,0:T(8,128)(2,1)} %get-tuple-element.14), channel_id=1, source_target_pairs={{0,12},{2,14},{4,0},{6,2},{8,4},{10,6},{12,8},{14,10},{1,13},{3,15... | collective-permute-start | bytes 589832 | tf_op jit(solution)/shard_map/ppermute | solution.py:32
  60.5 11.9 %collective-permute-done.3 = bf16[2,192,256]{2,1,0:T(8,128)(2,1)} collective-permute-done((bf16[2,192,256]{2,1,0:T(8,128)(2,1)S(1)}, bf16[2,192,256]{2,1,0:T(8,128)(2,1)}, u32[]{:S(2)}, u32[]{:S(2)}) %collective-permute-start.3) | collective-permute-done | bytes 196640 | tf_op jit(solution)/shard_map/ppermute | solution.py:32
  72.4 1.9 %collective-permute-start = (bf16[256,3072]{1,0:T(8,128)(2,1)}, bf16[256,3072]{1,0:T(8,128)(2,1)S(1)}, u32[]{:S(2)}, u32[]{:S(2)}) collective-permute-start(bf16[256,3072]{1,0:T(8,128)(2,1)} %bitcast.2), channel_id=1, source_target_pairs={{0,1},{1,0},{2,3},{3,2},{4,5},{5,4},{6,7},{7,6},{8,9},{9,8},{10,11... | collective-permute-start | bytes 4718600 | tf_op jit(solution)/shard_map/ppermute | solution.py:67
  74.3 0.9 bitcast_dynamic-update-slice_fusion.5
  75.2 3.6 %collective-permute-start.6 = (bf16[2,192,256]{2,1,0:T(8,128)(2,1)}, bf16[2,192,256]{2,1,0:T(8,128)(2,1)S(1)}, u32[]{:S(2)}, u32[]{:S(2)}) collective-permute-start(bf16[2,192,256]{2,1,0:T(8,128)(2,1)} %get-tuple-element.15), channel_id=1, source_target_pairs={{0,6},{2,8},{4,10},{6,12},{8,14},{10,0},{12,2},{14,4},{1,7},{3,9},... | collective-permute-start | bytes 589832 | tf_op jit(solution)/shard_map/ppermute | solution.py:32
  78.8 0.9 bitcast_dynamic-update-slice_fusion.4
  80.4 15.7 %collective-permute-done.6 = bf16[2,192,256]{2,1,0:T(8,128)(2,1)S(1)} collective-permute-done((bf16[2,192,256]{2,1,0:T(8,128)(2,1)}, bf16[2,192,256]{2,1,0:T(8,128)(2,1)S(1)}, u32[]{:S(2)}, u32[]{:S(2)}) %collective-permute-start.6) | collective-permute-done | bytes 196640 | tf_op jit(solution)/shard_map/ppermute | solution.py:32
  97.1 0.9 bitcast_dynamic-update-slice_fusion
  98.6 1.5 convolution_add_fusion.2
  100.1 1.4 broadcast_select_fusion.1
  103.7 1.3 convolution_convert_fusion.1
  106.8 2.5 %maximum_bitcast_fusion.1 = bf16[8,256,384]{1,2,0:T(8,128)(2,1)} fusion(bf16[256,8,192]{0,2,1:T(8,128)(2,1)S(1)} %bitcast.103, bf16[256,8,192]{0,2,1:T(8,128)(2,1)} %convolution_convert_fusion.1), kind=kLoop, calls=%fused_computation.25 | loop fusion | flops 3145728 | bytes 3145728 | tf_op jit(solution)/shard_map/convert_element_type | solution.py:91
  109.3 2.2 %collective-permute-start.9 = (bf16[8,256,384]{1,2,0:T(8,128)(2,1)}, bf16[8,256,384]{1,2,0:T(8,128)(2,1)}, u32[]{:S(2)}, u32[]{:S(2)}) collective-permute-start(bf16[8,256,384]{1,2,0:T(8,128)(2,1)} %maximum_bitcast_fusion.1), channel_id=1, source_target_pairs={{0,1},{1,0},{2,3},{3,2},{4,5},{5,4},{6,7},{7,6},{8,9},{9,8},{10,11... | collective-permute-start | bytes 4718600 | tf_op jit(solution)/shard_map/ppermute | solution.py:93
  112.0 1.6 convolution_add_fusion.1
  113.5 1.9 %copy.66 = f32[256,1536]{0,1:T(8,128)S(1)} copy(f32[256,1536]{1,0:T(8,128)} %convolution_add_fusion.1) | data formatting | bytes 3145728 | tf_op jit(solution)/shard_map/add | solution.py:88
  115.9 1.8 fusion.1
  117.6 44.5 %all_to_all.15 = bf16[8,256,384]{1,2,0:T(8,128)(2,1)S(1)} all-to-all(bf16[8,256,384]{1,2,0:T(8,128)(2,1)S(1)} %fusion.1), channel_id=1, replica_groups=mesh['x'=4,'z'=8,'y'=8,'c'=2] {'y'}, dimensions={0} | all-to-all | bytes 3145728 | tf_op jit(solution)/shard_map/all_to_all | solution.py:94
  163.2 9.8 %all-to-all-start.2 = ((bf16[32,8,384]{2,1,0:T(8,128)(2,1)}), bf16[32,8,384]{2,1,0:T(8,128)(2,1)S(1)}, u32[]{:S(2)}, u32[]{:S(2)}) async-start(bf16[32,8,384]{2,1,0:T(8,128)(2,1)} %bitcast.39), calls=%async_computation.2 | async-start | bytes 393216 | tf_op jit(solution)/shard_map/all_to_all | solution.py:97
  173.1 10.3 %all-to-all-done.2 = bf16[32,8,384]{2,1,0:T(8,128)(2,1)S(1)} async-done(((bf16[32,8,384]{2,1,0:T(8,128)(2,1)}), bf16[32,8,384]{2,1,0:T(8,128)(2,1)S(1)}, u32[]{:S(2)}, u32[]{:S(2)}) %all-to-all-start.2) | async-done | bytes 196640 | tf_op jit(solution)/shard_map/all_to_all | solution.py:97
  (72 shorter events, 15.8 us)
Async XLA Ops:
  0.6 4.8 %copy-start = (bf16[16,3072]{1,0:T(8,128)(2,1)S(1)}, bf16[16,3072]{1,0:T(8,128)(2,1)}, u32[]{:S(2)}) copy-start(bf16[16,3072]{1,0:T(8,128)(2,1)} %param.7) | copy-start | bytes 294916
  7.1 13.7 %copy-start.6 = (bf16[4096,192]{0,1:T(8,128)(2,1)S(1)}, bf16[4096,192]{0,1:T(8,128)(2,1)}, u32[]{:S(2)}) copy-start(bf16[4096,192]{0,1:T(8,128)(2,1)} %param.13) | copy-start | bytes 4718596
  7.1 65.3 %all-to-all-start = ((bf16[32,8,3072]{2,1,0:T(8,128)(2,1)}), bf16[32,8,3072]{2,1,0:T(8,128)(2,1)}, u32[]{:S(2)}, u32[]{:S(2)}) async-start(bf16[32,8,3072]{2,1,0:T(8,128)(2,1)} %bitcast.1), calls=%async_computation | async-start | bytes 3145728 | tf_op jit(solution)/shard_map/all_to_all | solution.py:65
  26.4 3.5 %copy-start.1 = (bf16[192,8,1,256]{3,2,1,0:T(2,128)(2,1)S(1)}, bf16[192,8,1,256]{3,2,1,0:T(2,128)(2,1)}, u32[]{:S(2)}) copy-start(bf16[192,8,1,256]{3,2,1,0:T(2,128)(2,1)} %get-tuple-element.16) | copy-start | bytes 2359300
  27.7 6.3 %collective-permute-start.1 = (bf16[8,192,256]{2,1,0:T(8,128)(2,1)}, bf16[8,192,256]{2,1,0:T(8,128)(2,1)S(1)}, u32[]{:S(2)}, u32[]{:S(2)}) collective-permute-start(bf16[8,192,256]{2,1,0:T(8,128)(2,1)} %bitcast.94), channel_id=1, source_target_pairs={{0,1},{1,0},{2,3},{3,2},{4,5},{5,4},{6,7},{7,6},{8,9},{9,8},{10,11... | collective-permute-start | bytes 2359304 | tf_op jit(solution)/shard_map/ppermute | solution.py:26
  34.9 21.9 %collective-permute-start.2 = (bf16[2,192,256]{2,1,0:T(8,128)(2,1)S(1)}, bf16[2,192,256]{2,1,0:T(8,128)(2,1)S(1)}, u32[]{:S(2)}, u32[]{:S(2)}) collective-permute-start(bf16[2,192,256]{2,1,0:T(8,128)(2,1)S(1)} %get-tuple-element.11), channel_id=1, source_target_pairs={{0,2},{2,4},{4,6},{6,8},{8,10},{10,12},{12,14},{14,0},{1,3},{3,5},... | collective-permute-start | bytes 589832 | tf_op jit(solution)/shard_map/ppermute | solution.py:32
  39.1 57.1 %collective-permute-start.7 = (bf16[2,192,256]{2,1,0:T(8,128)(2,1)}, bf16[2,192,256]{2,1,0:T(8,128)(2,1)}, u32[]{:S(2)}, u32[]{:S(2)}) collective-permute-start(bf16[2,192,256]{2,1,0:T(8,128)(2,1)} %fusion.21), channel_id=1, source_target_pairs={{0,10},{2,12},{4,14},{6,0},{8,2},{10,4},{12,6},{14,8},{1,11},{3,13... | collective-permute-start | bytes 589832 | tf_op jit(solution)/shard_map/ppermute | solution.py:32
  45.1 52.0 %collective-permute-start.8 = (bf16[2,192,256]{2,1,0:T(8,128)(2,1)S(1)}, bf16[2,192,256]{2,1,0:T(8,128)(2,1)}, u32[]{:S(2)}, u32[]{:S(2)}) collective-permute-start(bf16[2,192,256]{2,1,0:T(8,128)(2,1)S(1)} %get-tuple-element.10), channel_id=1, source_target_pairs={{0,8},{2,10},{4,12},{6,14},{8,0},{10,2},{12,4},{14,6},{1,9},{3,11}... | collective-permute-start | bytes 589832 | tf_op jit(solution)/shard_map/ppermute | solution.py:32
  48.9 23.4 %collective-permute-start.3 = (bf16[2,192,256]{2,1,0:T(8,128)(2,1)S(1)}, bf16[2,192,256]{2,1,0:T(8,128)(2,1)}, u32[]{:S(2)}, u32[]{:S(2)}) collective-permute-start(bf16[2,192,256]{2,1,0:T(8,128)(2,1)S(1)} %get-tuple-element.12), channel_id=1, source_target_pairs={{0,14},{2,0},{4,2},{6,4},{8,6},{10,8},{12,10},{14,12},{1,15},{3,1}... | collective-permute-start | bytes 589832 | tf_op jit(solution)/shard_map/ppermute | solution.py:32
  52.3 22.9 %collective-permute-start.4 = (bf16[2,192,256]{2,1,0:T(8,128)(2,1)}, bf16[2,192,256]{2,1,0:T(8,128)(2,1)}, u32[]{:S(2)}, u32[]{:S(2)}) collective-permute-start(bf16[2,192,256]{2,1,0:T(8,128)(2,1)} %get-tuple-element.13), channel_id=1, source_target_pairs={{0,4},{2,6},{4,8},{6,10},{8,12},{10,14},{12,0},{14,2},{1,5},{3,7},... | collective-permute-start | bytes 589832 | tf_op jit(solution)/shard_map/ppermute | solution.py:32
  56.8 23.6 %collective-permute-start.5 = (bf16[2,192,256]{2,1,0:T(8,128)(2,1)}, bf16[2,192,256]{2,1,0:T(8,128)(2,1)S(1)}, u32[]{:S(2)}, u32[]{:S(2)}) collective-permute-start(bf16[2,192,256]{2,1,0:T(8,128)(2,1)} %get-tuple-element.14), channel_id=1, source_target_pairs={{0,12},{2,14},{4,0},{6,2},{8,4},{10,6},{12,8},{14,10},{1,13},{3,15... | collective-permute-start | bytes 589832 | tf_op jit(solution)/shard_map/ppermute | solution.py:32
  72.4 25.8 %collective-permute-start = (bf16[256,3072]{1,0:T(8,128)(2,1)}, bf16[256,3072]{1,0:T(8,128)(2,1)S(1)}, u32[]{:S(2)}, u32[]{:S(2)}) collective-permute-start(bf16[256,3072]{1,0:T(8,128)(2,1)} %bitcast.2), channel_id=1, source_target_pairs={{0,1},{1,0},{2,3},{3,2},{4,5},{5,4},{6,7},{7,6},{8,9},{9,8},{10,11... | collective-permute-start | bytes 4718600 | tf_op jit(solution)/shard_map/ppermute | solution.py:67
  75.2 20.9 %collective-permute-start.6 = (bf16[2,192,256]{2,1,0:T(8,128)(2,1)}, bf16[2,192,256]{2,1,0:T(8,128)(2,1)S(1)}, u32[]{:S(2)}, u32[]{:S(2)}) collective-permute-start(bf16[2,192,256]{2,1,0:T(8,128)(2,1)} %get-tuple-element.15), channel_id=1, source_target_pairs={{0,6},{2,8},{4,10},{6,12},{8,14},{10,0},{12,2},{14,4},{1,7},{3,9},... | collective-permute-start | bytes 589832 | tf_op jit(solution)/shard_map/ppermute | solution.py:32
  100.1 1.6 copy-start.7
  101.7 1.4 copy-start.8
  103.7 1.3 copy-start.9
  103.7 1.3 copy-start.3
  105.0 1.1 copy-start.4
  106.8 4.7 %copy-start.2 = (bf16[8,1,192,256]{3,2,1,0:T(8,128)(2,1)S(1)}, bf16[8,1,192,256]{3,2,1,0:T(8,128)(2,1)}, u32[]{:S(2)}) copy-start(bf16[8,1,192,256]{3,2,1,0:T(8,128)(2,1)} %get-tuple-element.21) | copy-start | bytes 2359300
  109.3 2.6 %copy-start.5 = (bf16[8,1,192,256]{3,2,1,0:T(8,128)(2,1)S(1)}, bf16[8,1,192,256]{3,2,1,0:T(8,128)(2,1)}, u32[]{:S(2)}) copy-start(bf16[8,1,192,256]{3,2,1,0:T(8,128)(2,1)} %get-tuple-element.5) | copy-start | bytes 2359300
  109.3 6.5 %collective-permute-start.9 = (bf16[8,256,384]{1,2,0:T(8,128)(2,1)}, bf16[8,256,384]{1,2,0:T(8,128)(2,1)}, u32[]{:S(2)}, u32[]{:S(2)}) collective-permute-start(bf16[8,256,384]{1,2,0:T(8,128)(2,1)} %maximum_bitcast_fusion.1), channel_id=1, source_target_pairs={{0,1},{1,0},{2,3},{3,2},{4,5},{5,4},{6,7},{7,6},{8,9},{9,8},{10,11... | collective-permute-start | bytes 4718600 | tf_op jit(solution)/shard_map/ppermute | solution.py:93
  113.5 1.9 %copy-start.10 = (bf16[256,256,1]{1,0,2:T(8,128)(2,1)S(1)}, bf16[256,256,1]{1,0,2:T(8,128)(2,1)}, u32[]{:S(2)}) copy-start(bf16[256,256,1]{1,0,2:T(8,128)(2,1)} %copy-done.9) | copy-start | bytes 393220
  162.1 10.9 %copy-start.11 = (f32[16,2]{0,1:T(2,128)S(1)}, f32[16,2]{0,1:T(2,128)}, u32[]{:S(2)}) copy-start(f32[16,2]{0,1:T(2,128)} %param.10) | copy-start | bytes 388
  163.2 20.2 %all-to-all-start.2 = ((bf16[32,8,384]{2,1,0:T(8,128)(2,1)}), bf16[32,8,384]{2,1,0:T(8,128)(2,1)S(1)}, u32[]{:S(2)}, u32[]{:S(2)}) async-start(bf16[32,8,384]{2,1,0:T(8,128)(2,1)} %bitcast.39), calls=%async_computation.2 | async-start | bytes 393216 | tf_op jit(solution)/shard_map/all_to_all | solution.py:97

commit v2 on v1

v2 whole, which is shorter than its diff:
```python
import jax
import jax.numpy as jnp
from jax import lax
from jax.experimental import pallas as pl
from jax.experimental.pallas import tpu as pltpu
from jax.sharding import Mesh, PartitionSpec as P

EXPERTS = 8
CAP = 8
DP = ("x", "z")
SWAP = ((0, 1), (1, 0))
F32, BF16 = jnp.float32, jnp.bfloat16
VMEM = pl.BlockSpec(memory_space=pltpu.VMEM)
HBM = pl.BlockSpec(memory_space=pltpu.MemorySpace.HBM)
SMEM = pl.BlockSpec(memory_space=pltpu.SMEM)


def params(mib):
    return pltpu.CompilerParams(vmem_limit_bytes=mib * 2**20)


ROWS = 8
SHIFTS = (4, 3, 5, 2, 6, 1, 7)


def pin(a):
    return pltpu.with_memory_space_constraint(a, pltpu.MemorySpace.HBM)


def mm(a, b):
    return jnp.dot(a, b, preferred_element_type=F32)


def mm_t(a, b):
    return lax.dot_general(a, b, (((1,), (1,)), ((), ())), preferred_element_type=F32)


def shape(*dims, dtype=BF16):
    return jax.ShapeDtypeStruct(dims, dtype)


def slot_table(routes, gates, by_token):
    slots = EXPERTS * CAP
    count_tok = routes.shape[0] if by_token else routes.shape[1]
    dims, axis = ((count_tok, slots), 1) if by_token else ((slots, count_tok), 0)
    pick = (lambda a, k: a[:, k : k + 1]) if by_token else (lambda a, k: a[k : k + 1, :])
    slot = lax.broadcasted_iota(jnp.int32, dims, axis)
    first, second = pick(routes, 0) == slot // CAP, pick(routes, 1) == slot // CAP
    member = jnp.where(first | second, 1.0, 0.0).astype(BF16)
    a = lax.broadcasted_iota(jnp.int32, (count_tok, count_tok), axis)
    b = lax.broadcasted_iota(jnp.int32, (count_tok, count_tok), 1 - axis)
    earlier = jnp.where(a < b, 1.0, 0.0).astype(BF16)
    rank = mm(earlier, member) if by_token else mm(member, earlier)
    mine = jnp.where((rank == (slot % CAP).astype(F32)) & (first | second), 1.0, 0.0)
    gate = jnp.where(first, pick(gates, 0), 0.0) + jnp.where(second, pick(gates, 1), 0.0)
    return mine, mine * gate


def first_kernel(at_ref, tokens_hbm, cot_hbm, routes_hbm, gates_hbm, gate_hbm, up_hbm, down_hbm, sent_ref, *rest):
    cut, away_hbm, held, sems = rest[: ROWS - 1], rest[ROWS - 1], rest[ROWS : ROWS + 4], rest[ROWS + 4]
    cols, width = cut[0].shape
    moves = list(zip((tokens_hbm, cot_hbm, routes_hbm, gates_hbm), held))
    for i, source in enumerate((gate_hbm, up_hbm)):
        for y in range(ROWS):
            rows = pl.ds(pl.multiple_of((2 * y + 1 - at_ref[0]) * cols, cols), cols)
            moves.append((source.at[rows], away_hbm.at[i, pl.ds(y * cols, cols)]))
    for shift, to in zip(SHIFTS, cut):
        y = lax.rem(at_ref[1] + shift, ROWS)
        moves.append((down_hbm.at[:, pl.ds(pl.multiple_of(y * width, width), width)], to))
    copies = [pltpu.make_async_copy(*move, sems.at[i]) for i, move in enumerate(moves)]
    for copy in copies:
        copy.start()
    for copy in copies[:4]:
        copy.wait()
    tokens_ref, cot_ref, routes_ref, gates_ref = held
    model = tokens_ref.shape[1]
    half = model // 2
    low = at_ref[0] == 0
    mine, gate = slot_table(routes_ref[...], gates_ref[...], False)
    gate = jnp.sum(gate, axis=1, keepdims=True)
    mine = mine.astype(BF16)

    def ours(ref):
        cut = [ref[:, i * cols : (i + 1) * cols] for i in range(2 * ROWS)]
        return jnp.concatenate([jnp.where(low, cut[2 * y], cut[2 * y + 1]) for y in range(ROWS)], axis=1)

    x = mm(mine, ours(tokens_ref)).reshape(EXPERTS, CAP, half).astype(BF16)
    dy = (mm(mine, ours(cot_ref)) * gate).reshape(EXPERTS, CAP, half).astype(BF16)
    for copy in range(sent_ref.shape[1]):
        sent_ref[:, copy, :, :half] = x
        sent_ref[:, copy, :, half:] = dy
    for copy in copies[4:]:
        copy.wait()


def weight_copies(at_ref, gate_hbm, up_hbm, far_hbm, down_hbm, pieces, gate_w, up_w, down_w, sems):
    cols, width = gate_w.shape[1], gate_w.shape[2] // 2
    steps = []
    for i, shift in enumerate((0, *SHIFTS)):
        y = lax.rem(at_ref[1] - shift + ROWS, ROWS)
        rows = pl.ds(pl.multiple_of((2 * y + at_ref[0]) * cols, cols), cols)
        far = pl.ds(pl.multiple_of(y * cols, cols), cols)
        own_units = pl.ds(pl.multiple_of(at_ref[1] * 2 * width, 2 * width), 2 * width)
        moves = [
            (gate_hbm.at[rows], gate_w.at[y, :, pl.ds(0, width)]),
            (far_hbm.at[0, far], gate_w.at[y, :, pl.ds(width, width)]),
            (up_hbm.at[rows], up_w.at[y, :, pl.ds(0, width)]),
            (far_hbm.at[1, far], up_w.at[y, :, pl.ds(width, width)]),
            (down_hbm.at[:, own_units] if shift == 0 else pieces[i - 1], down_w.at[y]),
        ]
        copies = [pltpu.make_async_copy(*move, sems.at[5 * i + j]) for j, move in enumerate(moves)]
        steps.append((y, copies))
    return steps


def before_kernel(at_ref, got_ref, gate_hbm, up_hbm, far_hbm, down_hbm, *rest):
    pieces, (keep_ref, send_ref, gate_w, up_w, down_w, sems) = rest[: ROWS - 1], rest[ROWS - 1 :]
    steps = weight_copies(at_ref, gate_hbm, up_hbm, far_hbm, down_hbm, pieces, gate_w, up_w, down_w, sems)
    for j in range(5):
        for _, copies in steps:
            copies[j].start()
    low = at_ref[0] == 0
    half = got_ref.shape[1] // 2
    width = keep_ref.shape[2]
    for i, (weight, part, needs) in enumerate(((gate_w, 0, (0, 1)), (up_w, 0, (2, 3)), (down_w, 1, (4,)))):
        for _, copies in steps:
            for j in needs:
                copies[j].wait()
        both = mm(got_ref[:, part * half : (part + 1) * half], weight[...].reshape(half, 2 * width))
        left, right = both[:, :width], both[:, width:]
        if part:
            left, right = jnp.where(low, left, right), jnp.where(low, right, left)
        keep_ref[i] = left
        send_ref[i] = right


def middle_kernel(keep_ref, came_ref, act_ref):
    gate_pre, up_pre, d_hidden = (keep_ref[i] + came_ref[i] for i in range(3))
    s = jax.nn.sigmoid(gate_pre)
    activated = gate_pre * s
    act_ref[0] = (activated * up_pre).astype(BF16)
    act_ref[1] = (d_hidden * up_pre * s * (1.0 + gate_pre * (1.0 - s))).astype(BF16)
    act_ref[2] = (d_hidden * activated).astype(BF16)


def after_kernel(at_ref, act_ref, came_ref, gate_w, up_w, down_w, sent_ref):
    low = at_ref[0] == 0
    block = 2 * gate_w.shape[1]
    hidden = jnp.concatenate(
        [jnp.where(low, act_ref[0], came_ref[0]), jnp.where(low, came_ref[0], act_ref[0])], axis=1
    )
    d_gate = jnp.concatenate([act_ref[1], came_ref[1]], axis=1)
    d_up = jnp.concatenate([act_ref[2], came_ref[2]], axis=1)
    for y in range(ROWS):
        out = mm_t(hidden, down_w[y])
        grad = mm_t(d_gate, gate_w[y]) + mm_t(d_up, up_w[y])
        sent_ref[:, y * block : (y + 1) * block] = jnp.concatenate([out, grad], axis=1).astype(BF16)


def combine_kernel(back_ref, routes_ref, gates_ref, mixed_ref):
    cols = mixed_ref.shape[2] // 2
    summed = back_ref[:, 0].astype(F32)
    for copy in range(1, back_ref.shape[1]):
        summed = summed + back_ref[:, copy].astype(F32)
    summed = summed.reshape(EXPERTS * CAP, -1)
    mine, gate = slot_table(routes_ref[...], gates_ref[...], True)

    def pick(weights, values):
        return jnp.dot(weights, values, precision=lax.Precision.HIGHEST, preferred_element_type=F32)

    for y in range(ROWS):
        out = pick(gate, summed[:, 2 * y * cols : (2 * y + 1) * cols])
        grad = pick(mine, summed[:, (2 * y + 1) * cols : 2 * (y + 1) * cols])
        mixed_ref[y] = jnp.concatenate([out, grad], axis=1).astype(BF16)


def call(kernel, out_shape, *args, scalars=0, mib=8):
    single = not isinstance(out_shape, list)
    return pl.pallas_call(
        kernel,
        in_specs=[SMEM] * scalars + [VMEM] * (len(args) - scalars),
        out_specs=VMEM if single else [VMEM] * len(out_shape),
        out_shape=out_shape,
        compiler_params=params(mib),
    )(*args)


def body(tokens, cotangent, routes, gates, w_gate, w_up, w_down):
    count_tok, model = tokens.shape
    n_dp = lax.axis_size(DP)
    copies = n_dp // EXPERTS
    cols, width = w_down.shape[1], w_gate.shape[1]
    lines, half = n_dp * CAP, model // 2
    at = jnp.stack([lax.axis_index("c"), lax.axis_index("y")]).astype(jnp.int32)
    down = w_down.T

    held = (tokens, cotangent, routes.T, gates.T)
    sent, *cut, away = pl.pallas_call(
        first_kernel,
        in_specs=[SMEM] + [HBM] * 7,
        out_specs=[VMEM] + [HBM] * ROWS,
        out_shape=[shape(EXPERTS, copies, CAP, model)]
        + [shape(cols, 2 * width)] * (ROWS - 1)
        + [shape(2, half, width)],
        scratch_shapes=[pltpu.VMEM(a.shape, a.dtype) for a in held]
        + [pltpu.SemaphoreType.DMA((4 + 2 * ROWS + ROWS - 1,))],
        compiler_params=params(8),
    )(at, *(pin(a) for a in (*held, w_gate, w_up, down)))
    got = lax.all_to_all(sent.reshape(n_dp, CAP, model), DP, split_axis=0, concat_axis=0, tiled=True)

    far = lax.ppermute(away, "c", SWAP)
    *late, far = lax.optimization_barrier((*cut[4:], far))
    cut = tuple(pin(a) for a in (*cut[:4], *late))
    pieces = [lax.ppermute(a, "y", [(i, (i + s) % ROWS) for i in range(ROWS)]) for a, s in zip(cut, SHIFTS)]

    got, *pieces = lax.optimization_barrier((got, *pieces))
    keep, send, *weights = pl.pallas_call(
        before_kernel,
        in_specs=[SMEM, VMEM] + [HBM] * (3 + ROWS),
        out_specs=[VMEM] * 5,
        out_shape=[shape(3, lines, width, dtype=F32)] * 2 + [shape(ROWS, cols, 2 * width)] * 3,
        scratch_shapes=[pltpu.SemaphoreType.DMA((5 * ROWS,))],
        compiler_params=params(8),
    )(at, got.reshape(lines, model), *(pin(a) for a in (w_gate, w_up, far, down, *pieces)))
    act = call(middle_kernel, shape(3, lines, width), keep, lax.ppermute(send, "c", SWAP))
    sent = call(after_kernel, shape(lines, model), at, act, lax.ppermute(act, "c", SWAP), *weights, scalars=1)
    back = lax.all_to_all(sent.reshape(n_dp, CAP, model), DP, split_axis=0, concat_axis=0, tiled=True)
    mixed = call(
        combine_kernel,
        shape(ROWS, count_tok, 2 * cols),
        back.reshape(EXPERTS, copies, CAP, model), routes, gates,
    )
    mixed = lax.all_to_all(mixed, "y", split_axis=0, concat_axis=0, tiled=True)
    mixed = jnp.sum(mixed.astype(F32), axis=0).astype(BF16)
    return mixed[:, :cols], mixed[:, cols:]


def solution(mesh):
    size = dict(x=4, z=8, y=ROWS, c=2)
    fine = Mesh(mesh.devices.reshape(tuple(size.values())), tuple(size))
    dp, tensor = DP, ("y", "c")
    placed = (P(dp, None),) * 4 + (P(None, dp + tensor),) * 2 + (P(dp, tensor),)
    return jax.shard_map(
        body,
        mesh=fine,
        in_specs=placed,
        out_specs=(P(dp, tensor), P(dp, tensor)),
        check_vma=False,
    )
```

time: 186 us -> 147 us (0.79)
  the two profiles are of different devices: /device:TPU:2 before, /device:TPU:8 now
where the time goes in v2:
time: 147 us
  waiting for transfers between devices  58.7 us (40%)
  starting transfers between devices  56.6 us (39%)
  Pallas kernels  12.7 us (9%)
  blocking collectives  12.7 us (9%)
  local copies, waits for them, and re-layouts  4.91 us (3%)
    all_to_all x2, waiting for transfers between devices, body(): lax.all_to_all(sent.reshape(n_dp, CAP, model), DP, split_axis=0, concat_a...  39.4 us
    ppermute x7, starting transfers between devices, body(): lax.ppermute(a, 'y', [(i, (i + s) % ROWS) for i in range(ROWS)])  27.6 us
    all_to_all x2, starting transfers between devices, body(): lax.all_to_all(sent.reshape(n_dp, CAP, model), DP, split_axis=0, concat_a...  23.1 us
    ppermute x7, waiting for transfers between devices, body(): lax.ppermute(a, 'y', [(i, (i + s) % ROWS) for i in range(ROWS)])  15.5 us
    all_to_all x1, blocking collectives, body(): mixed = lax.all_to_all(mixed, 'y', split_axis=0, concat_axis=0, tiled=True)  12.7 us
    pallas_call x3, Pallas kernels, call(): pl.pallas_call(kernel, in_specs=[SMEM] * scalars + [VMEM] * (len(args) -...  4.67 us
    unnamed x32, local copies, waits for them, and re-layouts  4.23 us
    pallas_call x1, Pallas kernels, body(): pl.pallas_call(before_kernel, in_specs=[SMEM, VMEM] + [HBM] * (3 + ROWS),...  4.12 us
  transfers between devices with their start and end apart: 12, of which 6 were waited for; matrix products, arithmetic and copies ran while one was open for 0% of the time, Pallas kernels for 0%

profile of v2, /device:TPU:8, one launch (start us, length us, event | category | flops | bytes accessed | tf_op | source)
XLA Modules:
  0.0 146.6 jit_solution(4881654017234569802)
XLA Ops:
  0.7 3.9 %shard_map.86 = (bf16[8,4,8,3072]{3,2,1,0:T(8,128)(2,1)}, bf16[192,512]{1,0:T(8,128)(2,1)S(1)}, bf16[192,512]{1,0:T(8,128)(2,1)S(1)}, bf16[192,512]{1,0:T(8,128)...) custom-call(s32[2]{0:T(128)S(1)} %pad_add_fusion.at_ref, ...), custom_call_target="tpu_custom_call" | custom-call | tf_op jit(solution)/shard_map/pallas_call | solution.py:198
  4.7 0.7 copy-done
  5.3 0.7 copy-done.1
  6.0 0.7 copy-done.2
  6.7 0.7 copy-done.3
  7.3 0.7 copy-done.4
  8.0 13.2 %all-to-all-start = ((bf16[32,8,3072]{2,1,0:T(8,128)(2,1)}), bf16[32,8,3072]{2,1,0:T(8,128)(2,1)S(1)}, u32[]{:S(2)}, u32[]{:S(2)}) async-start(bf16[32,8,3072]{2,1,0:T(8,128)(2,1)} %bitcast.5), calls=%async_computation | async-start | bytes 3145728 | tf_op jit(solution)/shard_map/all_to_all | solution.py:209
  21.2 1.9 %collective-permute-start.4 = (bf16[2,1536,256]{2,1,0:T(8,128)(2,1)S(1)}, bf16[2,1536,256]{2,1,0:T(8,128)(2,1)S(1)}, u32[]{:S(2)}, u32[]{:S(2)}) collective-permute-start(bf16[2,1536,256]{2,1,0:T(8,128)(2,1)S(1)} %get-tuple-element.36), channel_id=1, source_target_pairs={{0,1},{1,0},{2,3},{3,2},{4,5},{5,4},{6,7},{7,6},{8,9},{9,8},{10,11... | collective-permute-start | bytes 4718600 | tf_op jit(solution)/shard_map/ppermute | solution.py:211
  23.1 6.8 %collective-permute-start = (bf16[192,512]{1,0:T(8,128)(2,1)}, bf16[192,512]{1,0:T(8,128)(2,1)S(1)}, u32[]{:S(2)}, u32[]{:S(2)}) collective-permute-start(bf16[192,512]{1,0:T(8,128)(2,1)} %copy-done.4), channel_id=1, source_target_pairs={{0,8},{2,10},{4,12},{6,14},{8,0},{10,2},{12,4},{14,6},{1,9},{3,11}... | collective-permute-start | bytes 589832 | tf_op jit(solution)/shard_map/ppermute | solution.py:214
  29.9 1.9 %collective-permute-start.1 = (bf16[192,512]{1,0:T(8,128)(2,1)}, bf16[192,512]{1,0:T(8,128)(2,1)S(1)}, u32[]{:S(2)}, u32[]{:S(2)}) collective-permute-start(bf16[192,512]{1,0:T(8,128)(2,1)} %copy-done.3), channel_id=1, source_target_pairs={{0,6},{2,8},{4,10},{6,12},{8,14},{10,0},{12,2},{14,4},{1,7},{3,9},... | collective-permute-start | bytes 589832 | tf_op jit(solution)/shard_map/ppermute | solution.py:214
  31.9 6.9 %collective-permute-start.2 = (bf16[192,512]{1,0:T(8,128)(2,1)}, bf16[192,512]{1,0:T(8,128)(2,1)S(1)}, u32[]{:S(2)}, u32[]{:S(2)}) collective-permute-start(bf16[192,512]{1,0:T(8,128)(2,1)} %copy-done.2), channel_id=1, source_target_pairs={{0,10},{2,12},{4,14},{6,0},{8,2},{10,4},{12,6},{14,8},{1,11},{3,13... | collective-permute-start | bytes 589832 | tf_op jit(solution)/shard_map/ppermute | solution.py:214
  38.8 1.9 %collective-permute-start.3 = (bf16[192,512]{1,0:T(8,128)(2,1)}, bf16[192,512]{1,0:T(8,128)(2,1)S(1)}, u32[]{:S(2)}, u32[]{:S(2)}) collective-permute-start(bf16[192,512]{1,0:T(8,128)(2,1)} %copy-done.1), channel_id=1, source_target_pairs={{0,4},{2,6},{4,8},{6,10},{8,12},{10,14},{12,0},{14,2},{1,5},{3,7},... | collective-permute-start | bytes 589832 | tf_op jit(solution)/shard_map/ppermute | solution.py:214
  40.8 6.0 %collective-permute-start.5 = (bf16[192,512]{1,0:T(8,128)(2,1)}, bf16[192,512]{1,0:T(8,128)(2,1)S(1)}, u32[]{:S(2)}, u32[]{:S(2)}) collective-permute-start(bf16[192,512]{1,0:T(8,128)(2,1)} %copy-done), channel_id=1, source_target_pairs={{0,12},{2,14},{4,0},{6,2},{8,4},{10,6},{12,8},{14,10},{1,13},{3,15... | collective-permute-start | bytes 589832 | tf_op jit(solution)/shard_map/ppermute | solution.py:214
  46.8 1.9 %collective-permute-start.6 = (bf16[192,512]{1,0:T(8,128)(2,1)S(1)}, bf16[192,512]{1,0:T(8,128)(2,1)S(1)}, u32[]{:S(2)}, u32[]{:S(2)}) collective-permute-start(bf16[192,512]{1,0:T(8,128)(2,1)S(1)} %get-tuple-element.38), channel_id=1, source_target_pairs={{0,2},{2,4},{4,6},{6,8},{8,10},{10,12},{12,14},{14,0},{1,3},{3,5},... | collective-permute-start | bytes 589832 | tf_op jit(solution)/shard_map/ppermute | solution.py:214
  48.7 4.7 %collective-permute-done.1.rest_1_ = bf16[192,512]{1,0:T(8,128)(2,1)S(1)} collective-permute-done((bf16[192,512]{1,0:T(8,128)(2,1)}, bf16[192,512]{1,0:T(8,128)(2,1)S(1)}, u32[]{:S(2)}, u32[]{:S(2)}) %collective-permute-start.1) | collective-permute-done | bytes 196640 | tf_op jit(solution)/shard_map/ppermute | solution.py:214
  53.5 2.0 %collective-permute-start.7 = (bf16[192,512]{1,0:T(8,128)(2,1)S(1)}, bf16[192,512]{1,0:T(8,128)(2,1)S(1)}, u32[]{:S(2)}, u32[]{:S(2)}) collective-permute-start(bf16[192,512]{1,0:T(8,128)(2,1)S(1)} %get-tuple-element.39), channel_id=1, source_target_pairs={{0,14},{2,0},{4,2},{6,4},{8,6},{10,8},{12,10},{14,12},{1,15},{3,1}... | collective-permute-start | bytes 589832 | tf_op jit(solution)/shard_map/ppermute | solution.py:214
  55.5 6.3 %collective-permute-done.3.rest_3_ = bf16[192,512]{1,0:T(8,128)(2,1)S(1)} collective-permute-done((bf16[192,512]{1,0:T(8,128)(2,1)}, bf16[192,512]{1,0:T(8,128)(2,1)S(1)}, u32[]{:S(2)}, u32[]{:S(2)}) %collective-permute-start.3) | collective-permute-done | bytes 196640 | tf_op jit(solution)/shard_map/ppermute | solution.py:214
  61.8 4.4 %collective-permute-done.6.rest_5_ = bf16[192,512]{1,0:T(8,128)(2,1)S(1)} collective-permute-done((bf16[192,512]{1,0:T(8,128)(2,1)S(1)}, bf16[192,512]{1,0:T(8,128)(2,1)S(1)}, u32[]{:S(2)}, u32[]{:S(2)}) %collective-permute-start.6) | collective-permute-done | bytes 196640 | tf_op jit(solution)/shard_map/ppermute | solution.py:214
  66.4 0.6 copy-done.11
  67.1 4.1 %shard_map.87 = (f32[3,256,256]{2,1,0:T(8,128)S(1)}, f32[3,256,256]{2,1,0:T(8,128)S(1)}, bf16[8,192,512]{2,1,0:T(8,128)(2,1)S(1)}, bf16[8,192,512]{2,1,0:T(8,128)(2,1)S(1)}, bf16[8,192,512]{2,1,0:T(8,128)(2,1)S(1)}) custom-call(s32[2]{0:T(128)S(1)} %pad_add_fusion.at_ref, bf16[256,3072]{1,0:T(8,128)(2,1)S(1)} %bitcast.9, bf16[3072,256]{1,0:T(8,128)(2,1)} %gate_hbm.3, ...), custom_call_target="tpu_custom_call" | custom-call | tf_op jit(solution)/shard_map/pallas_call | solution.py:217
  71.2 1.9 %collective-permute-start.8 = (f32[3,256,256]{2,1,0:T(8,128)S(1)}, f32[3,256,256]{2,1,0:T(8,128)S(1)}, u32[]{:S(2)}, u32[]{:S(2)}) collective-permute-start(f32[3,256,256]{2,1,0:T(8,128)S(1)} %get-tuple-element.50), channel_id=1, source_target_pairs={{0,1},{1,0},{2,3},{3,2},{4,5},{5,4},{6,7},{7,6},{8,9},{9,8},{10,11... | collective-permute-start | bytes 2359304 | tf_op jit(solution)/shard_map/ppermute | solution.py:225
  73.1 2.3 %collective-permute-done.8.came_ref = f32[3,256,256]{2,1,0:T(8,128)S(1)} collective-permute-done((f32[3,256,256]{2,1,0:T(8,128)S(1)}, f32[3,256,256]{2,1,0:T(8,128)S(1)}, u32[]{:S(2)}, u32[]{:S(2)}) %collective-permute-start.8) | collective-permute-done | bytes 786464 | tf_op jit(solution)/shard_map/ppermute | solution.py:225
  75.4 0.2 shard_map.88.act_ref
  75.6 2.0 %collective-permute-start.9 = (bf16[3,256,256]{2,1,0:T(8,128)(2,1)S(1)}, bf16[3,256,256]{2,1,0:T(8,128)(2,1)S(1)}, u32[]{:S(2)}, u32[]{:S(2)}) collective-permute-start(bf16[3,256,256]{2,1,0:T(8,128)(2,1)S(1)} %shard_map.88.act_ref), channel_id=1, source_target_pairs={{0,1},{1,0},{2,3},{3,2},{4,5},{5,4},{6,7},{7,6},{8,9},{9,8},{10,11... | collective-permute-start | bytes 1179656 | tf_op jit(solution)/shard_map/ppermute | solution.py:226
  77.6 1.6 %collective-permute-done.9.came_ref = bf16[3,256,256]{2,1,0:T(8,128)(2,1)S(1)} collective-permute-done((bf16[3,256,256]{2,1,0:T(8,128)(2,1)S(1)}, bf16[3,256,256]{2,1,0:T(8,128)(2,1)S(1)}, u32[]{:S(2)}, u32[]{:S(2)}) %collective-permute-start.9) | collective-permute-done | bytes 393248 | tf_op jit(solution)/shard_map/ppermute | solution.py:226
  79.2 3.6 %shard_map.89 = bf16[256,3072]{1,0:T(8,128)(2,1)} custom-call(s32[2]{0:T(128)S(1)} %pad_add_fusion.at_ref, bf16[3,256,256]{2,1,0:T(8,128)(2,1)S(1)} %shard_map.88.act_ref, bf16[3,256,256]{2,1,0:T(8,128)(2,1)S(1)} %collective-permute-done.9.came_ref, bf16[8,192,512]{2,1,0:T(8,128)(2,1)S(1)} %get-tuple-element.51.gate_w, ...), custom_call_target="tpu_custom_call" | custom-call | tf_op jit(solution)/shard_map/pallas_call | solution.py:179
  82.8 9.9 %all-to-all-start.1 = ((bf16[32,8,3072]{2,1,0:T(8,128)(2,1)}), bf16[32,8,3072]{2,1,0:T(8,128)(2,1)S(1)}, u32[]{:S(2)}, u32[]{:S(2)}) async-start(bf16[32,8,3072]{2,1,0:T(8,128)(2,1)} %bitcast.7), calls=%async_computation.1 | async-start | bytes 3145728 | tf_op jit(solution)/shard_map/all_to_all | solution.py:227
  92.8 0.1 copy.10.gates_ref
  92.9 39.4 %all-to-all-done.1 = bf16[32,8,3072]{2,1,0:T(8,128)(2,1)S(1)} async-done(((bf16[32,8,3072]{2,1,0:T(8,128)(2,1)}), bf16[32,8,3072]{2,1,0:T(8,128)(2,1)S(1)}, u32[]{:S(2)}, u32[]{:S(2)}) %all-to-all-start.1) | async-done | bytes 1572896 | tf_op jit(solution)/shard_map/all_to_all | solution.py:227
  132.4 0.8 shard_map.90
  133.2 12.7 %all_to_all.15 = bf16[8,16,384]{2,1,0:T(8,128)(2,1)S(1)} all-to-all(bf16[8,16,384]{2,1,0:T(8,128)(2,1)S(1)} %shard_map.90), channel_id=1, replica_groups=mesh['x'=4,'z'=8,'y'=8,'c'=2] {'y'}, dimensions={0} | all-to-all | bytes 196608 | tf_op jit(solution)/shard_map/all_to_all | solution.py:233
  145.9 0.7 fusion
  (33 shorter events, 0.3 us)
Async XLA Ops:
  4.7 0.7 copy-start
  5.3 0.7 copy-start.1
  6.0 0.7 copy-start.2
  6.7 0.7 copy-start.3
  7.3 0.7 copy-start.4
  8.0 58.4 %all-to-all-start = ((bf16[32,8,3072]{2,1,0:T(8,128)(2,1)}), bf16[32,8,3072]{2,1,0:T(8,128)(2,1)S(1)}, u32[]{:S(2)}, u32[]{:S(2)}) async-start(bf16[32,8,3072]{2,1,0:T(8,128)(2,1)} %bitcast.5), calls=%async_computation | async-start | bytes 3145728 | tf_op jit(solution)/shard_map/all_to_all | solution.py:209
  21.2 19.6 %collective-permute-start.4 = (bf16[2,1536,256]{2,1,0:T(8,128)(2,1)S(1)}, bf16[2,1536,256]{2,1,0:T(8,128)(2,1)S(1)}, u32[]{:S(2)}, u32[]{:S(2)}) collective-permute-start(bf16[2,1536,256]{2,1,0:T(8,128)(2,1)S(1)} %get-tuple-element.36), channel_id=1, source_target_pairs={{0,1},{1,0},{2,3},{3,2},{4,5},{5,4},{6,7},{7,6},{8,9},{9,8},{10,11... | collective-permute-start | bytes 4718600 | tf_op jit(solution)/shard_map/ppermute | solution.py:211
  23.1 23.7 %collective-permute-start = (bf16[192,512]{1,0:T(8,128)(2,1)}, bf16[192,512]{1,0:T(8,128)(2,1)S(1)}, u32[]{:S(2)}, u32[]{:S(2)}) collective-permute-start(bf16[192,512]{1,0:T(8,128)(2,1)} %copy-done.4), channel_id=1, source_target_pairs={{0,8},{2,10},{4,12},{6,14},{8,0},{10,2},{12,4},{14,6},{1,9},{3,11}... | collective-permute-start | bytes 589832 | tf_op jit(solution)/shard_map/ppermute | solution.py:214
  29.9 23.5 %collective-permute-start.1 = (bf16[192,512]{1,0:T(8,128)(2,1)}, bf16[192,512]{1,0:T(8,128)(2,1)S(1)}, u32[]{:S(2)}, u32[]{:S(2)}) collective-permute-start(bf16[192,512]{1,0:T(8,128)(2,1)} %copy-done.3), channel_id=1, source_target_pairs={{0,6},{2,8},{4,10},{6,12},{8,14},{10,0},{12,2},{14,4},{1,7},{3,9},... | collective-permute-start | bytes 589832 | tf_op jit(solution)/shard_map/ppermute | solution.py:214
  31.9 23.6 %collective-permute-start.2 = (bf16[192,512]{1,0:T(8,128)(2,1)}, bf16[192,512]{1,0:T(8,128)(2,1)S(1)}, u32[]{:S(2)}, u32[]{:S(2)}) collective-permute-start(bf16[192,512]{1,0:T(8,128)(2,1)} %copy-done.2), channel_id=1, source_target_pairs={{0,10},{2,12},{4,14},{6,0},{8,2},{10,4},{12,6},{14,8},{1,11},{3,13... | collective-permute-start | bytes 589832 | tf_op jit(solution)/shard_map/ppermute | solution.py:214
  38.8 23.0 %collective-permute-start.3 = (bf16[192,512]{1,0:T(8,128)(2,1)}, bf16[192,512]{1,0:T(8,128)(2,1)S(1)}, u32[]{:S(2)}, u32[]{:S(2)}) collective-permute-start(bf16[192,512]{1,0:T(8,128)(2,1)} %copy-done.1), channel_id=1, source_target_pairs={{0,4},{2,6},{4,8},{6,10},{8,12},{10,14},{12,0},{14,2},{1,5},{3,7},... | collective-permute-start | bytes 589832 | tf_op jit(solution)/shard_map/ppermute | solution.py:214
  40.8 25.5 %copy-start.5 = (bf16[2,1536,256]{2,1,0:T(8,128)(2,1)}, bf16[2,1536,256]{2,1,0:T(8,128)(2,1)S(1)}, u32[]{:S(2)}) copy-start(bf16[2,1536,256]{2,1,0:T(8,128)(2,1)S(1)} %collective-permute-done.4.far_hbm) | copy-start | bytes 4718596
  40.8 21.1 %collective-permute-start.5 = (bf16[192,512]{1,0:T(8,128)(2,1)}, bf16[192,512]{1,0:T(8,128)(2,1)S(1)}, u32[]{:S(2)}, u32[]{:S(2)}) collective-permute-start(bf16[192,512]{1,0:T(8,128)(2,1)} %copy-done), channel_id=1, source_target_pairs={{0,12},{2,14},{4,0},{6,2},{8,4},{10,6},{12,8},{14,10},{1,13},{3,15... | collective-permute-start | bytes 589832 | tf_op jit(solution)/shard_map/ppermute | solution.py:214
  46.8 19.5 %copy-start.6 = (bf16[192,512]{1,0:T(8,128)(2,1)}, bf16[192,512]{1,0:T(8,128)(2,1)S(1)}, u32[]{:S(2)}) copy-start(bf16[192,512]{1,0:T(8,128)(2,1)S(1)} %collective-permute-done.rest_0_) | copy-start | bytes 589828
  46.8 19.5 %collective-permute-start.6 = (bf16[192,512]{1,0:T(8,128)(2,1)S(1)}, bf16[192,512]{1,0:T(8,128)(2,1)S(1)}, u32[]{:S(2)}, u32[]{:S(2)}) collective-permute-start(bf16[192,512]{1,0:T(8,128)(2,1)S(1)} %get-tuple-element.38), channel_id=1, source_target_pairs={{0,2},{2,4},{4,6},{6,8},{8,10},{10,12},{12,14},{14,0},{1,3},{3,5},... | collective-permute-start | bytes 589832 | tf_op jit(solution)/shard_map/ppermute | solution.py:214
  53.5 12.8 %copy-start.7 = (bf16[192,512]{1,0:T(8,128)(2,1)}, bf16[192,512]{1,0:T(8,128)(2,1)S(1)}, u32[]{:S(2)}) copy-start(bf16[192,512]{1,0:T(8,128)(2,1)S(1)} %collective-permute-done.1.rest_1_) | copy-start | bytes 589828
  53.5 12.9 %collective-permute-start.7 = (bf16[192,512]{1,0:T(8,128)(2,1)S(1)}, bf16[192,512]{1,0:T(8,128)(2,1)S(1)}, u32[]{:S(2)}, u32[]{:S(2)}) collective-permute-start(bf16[192,512]{1,0:T(8,128)(2,1)S(1)} %get-tuple-element.39), channel_id=1, source_target_pairs={{0,14},{2,0},{4,2},{6,4},{8,6},{10,8},{12,10},{14,12},{1,15},{3,1}... | collective-permute-start | bytes 589832 | tf_op jit(solution)/shard_map/ppermute | solution.py:214
  55.5 10.8 %copy-start.8 = (bf16[192,512]{1,0:T(8,128)(2,1)}, bf16[192,512]{1,0:T(8,128)(2,1)S(1)}, u32[]{:S(2)}) copy-start(bf16[192,512]{1,0:T(8,128)(2,1)S(1)} %collective-permute-done.2.rest_2_) | copy-start | bytes 589828
  61.8 4.5 %copy-start.9 = (bf16[192,512]{1,0:T(8,128)(2,1)}, bf16[192,512]{1,0:T(8,128)(2,1)S(1)}, u32[]{:S(2)}) copy-start(bf16[192,512]{1,0:T(8,128)(2,1)S(1)} %collective-permute-done.3.rest_3_) | copy-start | bytes 589828
  61.8 4.5 %copy-start.10 = (bf16[192,512]{1,0:T(8,128)(2,1)}, bf16[192,512]{1,0:T(8,128)(2,1)S(1)}, u32[]{:S(2)}) copy-start(bf16[192,512]{1,0:T(8,128)(2,1)S(1)} %collective-permute-done.5.rest_4_) | copy-start | bytes 589828
  66.3 0.7 copy-start.11
  66.3 0.7 copy-start.12
  71.2 4.2 %collective-permute-start.8 = (f32[3,256,256]{2,1,0:T(8,128)S(1)}, f32[3,256,256]{2,1,0:T(8,128)S(1)}, u32[]{:S(2)}, u32[]{:S(2)}) collective-permute-start(f32[3,256,256]{2,1,0:T(8,128)S(1)} %get-tuple-element.50), channel_id=1, source_target_pairs={{0,1},{1,0},{2,3},{3,2},{4,5},{5,4},{6,7},{7,6},{8,9},{9,8},{10,11... | collective-permute-start | bytes 2359304 | tf_op jit(solution)/shard_map/ppermute | solution.py:225
  75.6 3.6 %collective-permute-start.9 = (bf16[3,256,256]{2,1,0:T(8,128)(2,1)S(1)}, bf16[3,256,256]{2,1,0:T(8,128)(2,1)S(1)}, u32[]{:S(2)}, u32[]{:S(2)}) collective-permute-start(bf16[3,256,256]{2,1,0:T(8,128)(2,1)S(1)} %shard_map.88.act_ref), channel_id=1, source_target_pairs={{0,1},{1,0},{2,3},{3,2},{4,5},{5,4},{6,7},{7,6},{8,9},{9,8},{10,11... | collective-permute-start | bytes 1179656 | tf_op jit(solution)/shard_map/ppermute | solution.py:226
  82.8 9.9 %copy-start.13 = (f32[16,2]{0,1:T(2,128)S(1)}, f32[16,2]{0,1:T(2,128)}, u32[]{:S(2)}) copy-start(f32[16,2]{0,1:T(2,128)} %param.10) | copy-start | bytes 388
  82.8 10.0 %copy-start.14 = (s32[16,2]{0,1:T(2,128)S(1)}, s32[16,2]{0,1:T(2,128)}, u32[]{:S(2)}) copy-start(s32[16,2]{0,1:T(2,128)} %param.9) | copy-start | bytes 388
  82.8 49.5 %all-to-all-start.1 = ((bf16[32,8,3072]{2,1,0:T(8,128)(2,1)}), bf16[32,8,3072]{2,1,0:T(8,128)(2,1)S(1)}, u32[]{:S(2)}, u32[]{:S(2)}) async-start(bf16[32,8,3072]{2,1,0:T(8,128)(2,1)} %bitcast.7), calls=%async_computation.1 | async-start | bytes 3145728 | tf_op jit(solution)/shard_map/all_to_all | solution.py:227

commit v3 on v2

--- a/solution.py
+++ b/solution.py
@@ -56,25 +56,17 @@
     return mine, mine * gate
 
 
-def first_kernel(at_ref, tokens_hbm, cot_hbm, routes_hbm, gates_hbm, gate_hbm, up_hbm, down_hbm, sent_ref, *rest):
-    cut, away_hbm, held, sems = rest[: ROWS - 1], rest[ROWS - 1], rest[ROWS : ROWS + 4], rest[ROWS + 4]
-    cols, width = cut[0].shape
-    moves = list(zip((tokens_hbm, cot_hbm, routes_hbm, gates_hbm), held))
-    for i, source in enumerate((gate_hbm, up_hbm)):
-        for y in range(ROWS):
-            rows = pl.ds(pl.multiple_of((2 * y + 1 - at_ref[0]) * cols, cols), cols)
-            moves.append((source.at[rows], away_hbm.at[i, pl.ds(y * cols, cols)]))
-    for shift, to in zip(SHIFTS, cut):
-        y = lax.rem(at_ref[1] + shift, ROWS)
-        moves.append((down_hbm.at[:, pl.ds(pl.multiple_of(y * width, width), width)], to))
+def outbox_kernel(at_ref, tokens_hbm, cot_hbm, routes_hbm, gates_hbm, sent_ref, *rest):
+    held, sems = rest[:4], rest[4]
+    moves = zip((tokens_hbm, cot_hbm, routes_hbm, gates_hbm), held)
     copies = [pltpu.make_async_copy(*move, sems.at[i]) for i, move in enumerate(moves)]
     for copy in copies:
         copy.start()
-    for copy in copies[:4]:
+    for copy in copies:
         copy.wait()
     tokens_ref, cot_ref, routes_ref, gates_ref = held
     model = tokens_ref.shape[1]
-    half = model // 2
+    half, cols = model // 2, model // ROWS // 2
     low = at_ref[0] == 0
     mine, gate = slot_table(routes_ref[...], gates_ref[...], False)
     gate = jnp.sum(gate, axis=1, keepdims=True)
@@ -89,7 +81,22 @@
     for copy in range(sent_ref.shape[1]):
         sent_ref[:, copy, :, :half] = x
         sent_ref[:, copy, :, half:] = dy
-    for copy in copies[4:]:
+
+def cut_kernel(at_ref, gate_hbm, up_hbm, down_hbm, *rest):
+    cut, away_ref, sems = rest[: ROWS - 1], rest[ROWS - 1], rest[ROWS]
+    cols, width = cut[0].shape
+    moves = []
+    for shift, to in zip(SHIFTS, cut):
+        y = lax.rem(at_ref[1] + shift, ROWS)
+        moves.append((down_hbm.at[:, pl.ds(pl.multiple_of(y * width, width), width)], to))
+    for i, source in enumerate((gate_hbm, up_hbm)):
+        for y in range(ROWS):
+            rows = pl.ds(pl.multiple_of((2 * y + 1 - at_ref[0]) * cols, cols), cols)
+            moves.append((source.at[rows], away_ref.at[i, pl.ds(y * cols, cols)]))
+    copies = [pltpu.make_async_copy(*move, sems.at[i]) for i, move in enumerate(moves)]
+    for copy in copies:
+        copy.start()
+    for copy in copies:
         copy.wait()
 
 
@@ -114,14 +121,14 @@
 
 
 def before_kernel(at_ref, got_ref, gate_hbm, up_hbm, far_hbm, down_hbm, *rest):
-    pieces, (keep_ref, send_ref, gate_w, up_w, down_w, sems) = rest[: ROWS - 1], rest[ROWS - 1 :]
+    pieces, (part_ref, gate_w, up_w, down_w, sems) = rest[: ROWS - 1], rest[ROWS - 1 :]
     steps = weight_copies(at_ref, gate_hbm, up_hbm, far_hbm, down_hbm, pieces, gate_w, up_w, down_w, sems)
     for j in range(5):
         for _, copies in steps:
             copies[j].start()
     low = at_ref[0] == 0
     half = got_ref.shape[1] // 2
-    width = keep_ref.shape[2]
+    width = part_ref.shape[2] // 2
     for i, (weight, part, needs) in enumerate(((gate_w, 0, (0, 1)), (up_w, 0, (2, 3)), (down_w, 1, (4,)))):
         for _, copies in steps:
             for j in needs:
@@ -130,27 +137,29 @@
         left, right = both[:, :width], both[:, width:]
         if part:
             left, right = jnp.where(low, left, right), jnp.where(low, right, left)
-        keep_ref[i] = left
-        send_ref[i] = right
-
-
-def middle_kernel(keep_ref, came_ref, act_ref):
-    gate_pre, up_pre, d_hidden = (keep_ref[i] + came_ref[i] for i in range(3))
+        part_ref[i, :, :width] = left
+        part_ref[i, :, width:] = right
+
+
+def activations(gate_pre, up_pre, d_hidden):
     s = jax.nn.sigmoid(gate_pre)
     activated = gate_pre * s
-    act_ref[0] = (activated * up_pre).astype(BF16)
-    act_ref[1] = (d_hidden * up_pre * s * (1.0 + gate_pre * (1.0 - s))).astype(BF16)
-    act_ref[2] = (d_hidden * activated).astype(BF16)
-
-
-def after_kernel(at_ref, act_ref, came_ref, gate_w, up_w, down_w, sent_ref):
+    return (
+        (activated * up_pre).astype(BF16),
+        (d_hidden * up_pre * s * (1.0 + gate_pre * (1.0 - s))).astype(BF16),
+        (d_hidden * activated).astype(BF16),
+    )
+
+
+def after_kernel(at_ref, part_ref, came_ref, gate_w, up_w, down_w, sent_ref):
     low = at_ref[0] == 0
     block = 2 * gate_w.shape[1]
-    hidden = jnp.concatenate(
-        [jnp.where(low, act_ref[0], came_ref[0]), jnp.where(low, came_ref[0], act_ref[0])], axis=1
-    )
-    d_gate = jnp.concatenate([act_ref[1], came_ref[1]], axis=1)
-    d_up = jnp.concatenate([act_ref[2], came_ref[2]], axis=1)
+    width = part_ref.shape[2] // 2
+    own = activations(*(part_ref[i, :, :width] + came_ref[i, :, width:] for i in range(3)))
+    far = activations(*(part_ref[i, :, width:] + came_ref[i, :, :width] for i in range(3)))
+    hidden = jnp.concatenate([jnp.where(low, own[0], far[0]), jnp.where(low, far[0], own[0])], axis=1)
+    d_gate = jnp.concatenate([own[1], far[1]], axis=1)
+    d_up = jnp.concatenate([own[2], far[2]], axis=1)
     for y in range(ROWS):
         out = mm_t(hidden, down_w[y])
         grad = mm_t(d_gate, gate_w[y]) + mm_t(d_up, up_w[y])
@@ -195,35 +204,39 @@
     down = w_down.T
 
     held = (tokens, cotangent, routes.T, gates.T)
-    sent, *cut, away = pl.pallas_call(
-        first_kernel,
-        in_specs=[SMEM] + [HBM] * 7,
-        out_specs=[VMEM] + [HBM] * ROWS,
-        out_shape=[shape(EXPERTS, copies, CAP, model)]
-        + [shape(cols, 2 * width)] * (ROWS - 1)
-        + [shape(2, half, width)],
-        scratch_shapes=[pltpu.VMEM(a.shape, a.dtype) for a in held]
-        + [pltpu.SemaphoreType.DMA((4 + 2 * ROWS + ROWS - 1,))],
-        compiler_params=params(8),
-    )(at, *(pin(a) for a in (*held, w_gate, w_up, down)))
+    sent = pl.pallas_call(
+        outbox_kernel,
+        in_specs=[SMEM] + [HBM] * 4,
+        out_specs=VMEM,
+        out_shape=pltpu.VMEM((EXPERTS, copies, CAP, model), BF16),
+        scratch_shapes=[pltpu.VMEM(a.shape, a.dtype) for a in held] + [pltpu.SemaphoreType.DMA((4,))],
+        compiler_params=params(4),
+    )(at, *(pin(a) for a in held))
     got = lax.all_to_all(sent.reshape(n_dp, CAP, model), DP, split_axis=0, concat_axis=0, tiled=True)
 
+    *cut, away = pl.pallas_call(
+        cut_kernel,
+        in_specs=[SMEM] + [HBM] * 3,
+        out_specs=[VMEM] * ROWS,
+        out_shape=[pltpu.VMEM((cols, 2 * width), BF16)] * (ROWS - 1) + [pltpu.VMEM((2, half, width), BF16)],
+        scratch_shapes=[pltpu.SemaphoreType.DMA((3 * ROWS - 1,))],
+        compiler_params=params(1),
+    )(at, pin(w_gate), pin(w_up), pin(down))
     far = lax.ppermute(away, "c", SWAP)
     *late, far = lax.optimization_barrier((*cut[4:], far))
-    cut = tuple(pin(a) for a in (*cut[:4], *late))
+    cut = (*cut[:4], *late)
     pieces = [lax.ppermute(a, "y", [(i, (i + s) % ROWS) for i in range(ROWS)]) for a, s in zip(cut, SHIFTS)]
 
     got, *pieces = lax.optimization_barrier((got, *pieces))
-    keep, send, *weights = pl.pallas_call(
+    part, *weights = pl.pallas_call(
         before_kernel,
         in_specs=[SMEM, VMEM] + [HBM] * (3 + ROWS),
-        out_specs=[VMEM] * 5,
-        out_shape=[shape(3, lines, width, dtype=F32)] * 2 + [shape(ROWS, cols, 2 * width)] * 3,
+        out_specs=[VMEM] * 4,
+        out_shape=[shape(3, lines, 2 * width, dtype=F32)] + [shape(ROWS, cols, 2 * width)] * 3,
         scratch_shapes=[pltpu.SemaphoreType.DMA((5 * ROWS,))],
         compiler_params=params(8),
     )(at, got.reshape(lines, model), *(pin(a) for a in (w_gate, w_up, far, down, *pieces)))
-    act = call(middle_kernel, shape(3, lines, width), keep, lax.ppermute(send, "c", SWAP))
-    sent = call(after_kernel, shape(lines, model), at, act, lax.ppermute(act, "c", SWAP), *weights, scalars=1)
+    sent = call(after_kernel, shape(lines, model), at, part, lax.ppermute(part, "c", SWAP), *weights, scalars=1)
     back = lax.all_to_all(sent.reshape(n_dp, CAP, model), DP, split_axis=0, concat_axis=0, tiled=True)
     mixed = call(
         combine_kernel,

time: 147 us -> 143 us (0.973)
  local copies, waits for them, and re-layouts: 4.91 us -> 1.55 us
  starting transfers between devices: 56.6 us -> 54.4 us
  Pallas kernels: 12.7 us -> 14.6 us
    unnamed x32 -> x20, local copies, waits for them, and re-layouts: 4.23 us -> 0.87 us
    ppermute x2 -> x1, starting transfers between devices: 3.97 us -> 1.92 us  [body(): lax.ppermute(part, 'c', SWAP)]
    pallas_call x1 -> x2, Pallas kernels: 3.94 us -> 5.73 us  [the longest x1 3.08 us: body(): pl.pallas_call(outbox_kernel, in_specs=[SMEM] + [HBM] * 4, out_specs=VMEM...]
    ppermute x2 -> x1, waiting for transfers between devices: 3.82 us -> 3.38 us  [body(): lax.ppermute(part, 'c', SWAP)]
    pallas_call x3 -> x2, Pallas kernels: 4.67 us -> 4.68 us  [call(): pl.pallas_call(kernel, in_specs=[SMEM] * scalars + [VMEM] * (len(args) -...]
  transfers between devices with their start and end apart: 12 -> 11, of which waited for: 6 -> 5; matrix products, arithmetic and copies ran while one was open for 0% -> 0% of each run, Pallas kernels for 0% -> 2%
where the time goes in v3:
time: 143 us; the launch traced here: 142 us
  waiting for transfers between devices  58.2 us (41%)
  starting transfers between devices  54.4 us (38%)
  Pallas kernels  14.6 us (10%)
  blocking collectives  12.7 us (9%)
  local copies, waits for them, and re-layouts  1.55 us (1%)
    all_to_all x2, waiting for transfers between devices, body(): lax.all_to_all(sent.reshape(n_dp, CAP, model), DP, split_axis=0, concat_a...  39.4 us
    ppermute x7, starting transfers between devices, body(): lax.ppermute(a, 'y', [(i, (i + s) % ROWS) for i in range(ROWS)])  27.5 us
    all_to_all x2, starting transfers between devices, body(): lax.all_to_all(sent.reshape(n_dp, CAP, model), DP, split_axis=0, concat_a...  23.1 us
    ppermute x7, waiting for transfers between devices, body(): lax.ppermute(a, 'y', [(i, (i + s) % ROWS) for i in range(ROWS)])  15.4 us
    all_to_all x1, blocking collectives, body(): mixed = lax.all_to_all(mixed, 'y', split_axis=0, concat_axis=0, tiled=True)  12.7 us
    pallas_call x2, Pallas kernels, call(): pl.pallas_call(kernel, in_specs=[SMEM] * scalars + [VMEM] * (len(args) -...  4.68 us
    pallas_call x1, Pallas kernels, body(): pl.pallas_call(before_kernel, in_specs=[SMEM, VMEM] + [HBM] * (3 + ROWS),...  4.18 us
    ppermute x1, waiting for transfers between devices, body(): lax.ppermute(part, 'c', SWAP)  3.38 us
  transfers between devices with their start and end apart: 11, of which 5 were waited for; matrix products, arithmetic and copies ran while one was open for 0% of the time, Pallas kernels for 2%

profile of v3, /device:TPU:8, one launch (start us, length us, event | category | flops | bytes accessed | tf_op | source)
XLA Modules:
  0.0 142.4 jit_solution(13291579694202011415)
XLA Ops:
  0.6 0.1 pad_add_fusion.at_ref
  0.7 3.1 %shard_map.86 = bf16[8,4,8,3072]{3,2,1,0:T(8,128)(2,1)} custom-call(s32[2]{0:T(128)S(1)} %pad_add_fusion.at_ref, bf16[16,3072]{1,0:T(8,128)(2,1)} %tokens_hbm.1, bf16[16,3072]{1,0:T(8,128)(2,1)} %cot_hbm.1, s32[2,16]{1,0:T(2,128)} %bitcast.14, f32[2,16]{1,0:T(2,128)} %bitcast.13), custom_call_target="tpu_custom_call" | custom-call | tf_op jit(solution)/shard_map/pallas_call | solution.py:207
  3.8 13.2 %all-to-all-start = ((bf16[32,8,3072]{2,1,0:T(8,128)(2,1)}), bf16[32,8,3072]{2,1,0:T(8,128)(2,1)S(1)}, u32[]{:S(2)}, u32[]{:S(2)}) async-start(bf16[32,8,3072]{2,1,0:T(8,128)(2,1)} %bitcast.4), calls=%async_computation | async-start | bytes 3145728 | tf_op jit(solution)/shard_map/all_to_all | solution.py:215
  17.0 2.6 %shard_map.87 = (bf16[192,512]{1,0:T(8,128)(2,1)S(1)}, bf16[192,512]{1,0:T(8,128)(2,1)S(1)}, bf16[192,512]{1,0:T(8,128)(2,1)S(1)}, bf16[192,512]{1,0:T(8,128)(2,...) custom-call(s32[2]{0:T(128)S(1)} %pad_add_fusion.at_ref, ...), custom_call_target="tpu_custom_call" | custom-call | tf_op jit(solution)/shard_map/pallas_call | solution.py:217
  19.6 1.9 %collective-permute-start.4 = (bf16[2,1536,256]{2,1,0:T(8,128)(2,1)S(1)}, bf16[2,1536,256]{2,1,0:T(8,128)(2,1)S(1)}, u32[]{:S(2)}, u32[]{:S(2)}) collective-permute-start(bf16[2,1536,256]{2,1,0:T(8,128)(2,1)S(1)} %get-tuple-element.33), channel_id=1, source_target_pairs={{0,1},{1,0},{2,3},{3,2},{4,5},{5,4},{6,7},{7,6},{8,9},{9,8},{10,11... | collective-permute-start | bytes 4718600 | tf_op jit(solution)/shard_map/ppermute | solution.py:225
  21.6 6.8 %collective-permute-start = (bf16[192,512]{1,0:T(8,128)(2,1)S(1)}, bf16[192,512]{1,0:T(8,128)(2,1)S(1)}, u32[]{:S(2)}, u32[]{:S(2)}) collective-permute-start(bf16[192,512]{1,0:T(8,128)(2,1)S(1)} %get-tuple-element.26), channel_id=1, source_target_pairs={{0,8},{2,10},{4,12},{6,14},{8,0},{10,2},{12,4},{14,6},{1,9},{3,11}... | collective-permute-start | bytes 589832 | tf_op jit(solution)/shard_map/ppermute | solution.py:228
  28.4 1.9 %collective-permute-start.1 = (bf16[192,512]{1,0:T(8,128)(2,1)S(1)}, bf16[192,512]{1,0:T(8,128)(2,1)S(1)}, u32[]{:S(2)}, u32[]{:S(2)}) collective-permute-start(bf16[192,512]{1,0:T(8,128)(2,1)S(1)} %get-tuple-element.27), channel_id=1, source_target_pairs={{0,6},{2,8},{4,10},{6,12},{8,14},{10,0},{12,2},{14,4},{1,7},{3,9},... | collective-permute-start | bytes 589832 | tf_op jit(solution)/shard_map/ppermute | solution.py:228
  30.3 6.9 %collective-permute-start.2 = (bf16[192,512]{1,0:T(8,128)(2,1)S(1)}, bf16[192,512]{1,0:T(8,128)(2,1)S(1)}, u32[]{:S(2)}, u32[]{:S(2)}) collective-permute-start(bf16[192,512]{1,0:T(8,128)(2,1)S(1)} %get-tuple-element.28), channel_id=1, source_target_pairs={{0,10},{2,12},{4,14},{6,0},{8,2},{10,4},{12,6},{14,8},{1,11},{3,13... | collective-permute-start | bytes 589832 | tf_op jit(solution)/shard_map/ppermute | solution.py:228
  37.3 1.9 %collective-permute-start.3 = (bf16[192,512]{1,0:T(8,128)(2,1)S(1)}, bf16[192,512]{1,0:T(8,128)(2,1)S(1)}, u32[]{:S(2)}, u32[]{:S(2)}) collective-permute-start(bf16[192,512]{1,0:T(8,128)(2,1)S(1)} %get-tuple-element.29), channel_id=1, source_target_pairs={{0,4},{2,6},{4,8},{6,10},{8,12},{10,14},{12,0},{14,2},{1,5},{3,7},... | collective-permute-start | bytes 589832 | tf_op jit(solution)/shard_map/ppermute | solution.py:228
  39.2 0.0 collective-permute-done.4.far_hbm
  39.2 6.0 %collective-permute-start.5 = (bf16[192,512]{1,0:T(8,128)(2,1)S(1)}, bf16[192,512]{1,0:T(8,128)(2,1)S(1)}, u32[]{:S(2)}, u32[]{:S(2)}) collective-permute-start(bf16[192,512]{1,0:T(8,128)(2,1)S(1)} %get-tuple-element.34), channel_id=1, source_target_pairs={{0,12},{2,14},{4,0},{6,2},{8,4},{10,6},{12,8},{14,10},{1,13},{3,15... | collective-permute-start | bytes 589832 | tf_op jit(solution)/shard_map/ppermute | solution.py:228
  45.3 0.0 collective-permute-done.rest_0_
  45.3 1.9 %collective-permute-start.6 = (bf16[192,512]{1,0:T(8,128)(2,1)S(1)}, bf16[192,512]{1,0:T(8,128)(2,1)S(1)}, u32[]{:S(2)}, u32[]{:S(2)}) collective-permute-start(bf16[192,512]{1,0:T(8,128)(2,1)S(1)} %get-tuple-element.35), channel_id=1, source_target_pairs={{0,2},{2,4},{4,6},{6,8},{8,10},{10,12},{12,14},{14,0},{1,3},{3,5},... | collective-permute-start | bytes 589832 | tf_op jit(solution)/shard_map/ppermute | solution.py:228
  47.2 4.5 %collective-permute-done.1.rest_1_ = bf16[192,512]{1,0:T(8,128)(2,1)S(1)} collective-permute-done((bf16[192,512]{1,0:T(8,128)(2,1)S(1)}, bf16[192,512]{1,0:T(8,128)(2,1)S(1)}, u32[]{:S(2)}, u32[]{:S(2)}) %collective-permute-start.1) | collective-permute-done | bytes 196640 | tf_op jit(solution)/shard_map/ppermute | solution.py:228
  51.7 1.9 %collective-permute-start.7 = (bf16[192,512]{1,0:T(8,128)(2,1)S(1)}, bf16[192,512]{1,0:T(8,128)(2,1)}, u32[]{:S(2)}, u32[]{:S(2)}) collective-permute-start(bf16[192,512]{1,0:T(8,128)(2,1)S(1)} %get-tuple-element.36), channel_id=1, source_target_pairs={{0,14},{2,0},{4,2},{6,4},{8,6},{10,8},{12,10},{14,12},{1,15},{3,1}... | collective-permute-start | bytes 589832 | tf_op jit(solution)/shard_map/ppermute | solution.py:228
  53.6 0.0 collective-permute-done.2.rest_2_
  53.7 6.4 %collective-permute-done.3.rest_3_ = bf16[192,512]{1,0:T(8,128)(2,1)S(1)} collective-permute-done((bf16[192,512]{1,0:T(8,128)(2,1)S(1)}, bf16[192,512]{1,0:T(8,128)(2,1)S(1)}, u32[]{:S(2)}, u32[]{:S(2)}) %collective-permute-start.3) | collective-permute-done | bytes 196640 | tf_op jit(solution)/shard_map/ppermute | solution.py:228
  60.1 0.0 collective-permute-done.5.rest_4_
  60.1 4.4 %collective-permute-done.6.rest_5_ = bf16[192,512]{1,0:T(8,128)(2,1)S(1)} collective-permute-done((bf16[192,512]{1,0:T(8,128)(2,1)S(1)}, bf16[192,512]{1,0:T(8,128)(2,1)S(1)}, u32[]{:S(2)}, u32[]{:S(2)}) %collective-permute-start.6) | collective-permute-done | bytes 196640 | tf_op jit(solution)/shard_map/ppermute | solution.py:228
  64.6 0.7 copy-done.6
  65.2 0.0 collective-permute-done.7.rest_6_
  65.3 4.2 %shard_map.88 = (f32[3,256,512]{2,1,0:T(8,128)S(1)}, bf16[8,192,512]{2,1,0:T(8,128)(2,1)S(1)}, bf16[8,192,512]{2,1,0:T(8,128)(2,1)S(1)}, bf16[8,192,512]{2,1,0:T(8,128)(2,1)S(1)}) custom-call(s32[2]{0:T(128)S(1)} %pad_add_fusion.at_ref, bf16[256,3072]{1,0:T(8,128)(2,1)S(1)} %bitcast.9, bf16[3072,256]{1,0:T(8,128)(2,1)} %gate_hbm.3, ...), custom_call_target="tpu_custom_call" | custom-call | tf_op jit(solution)/shard_map/pallas_call | solution.py:231
  69.5 1.9 %collective-permute-start.8 = (f32[3,256,512]{2,1,0:T(8,128)S(1)}, f32[3,256,512]{2,1,0:T(8,128)S(1)}, u32[]{:S(2)}, u32[]{:S(2)}) collective-permute-start(f32[3,256,512]{2,1,0:T(8,128)S(1)} %get-tuple-element.46.part_ref), channel_id=1, source_target_pairs={{0,1},{1,0},{2,3},{3,2},{4,5},{5,4},{6,7},{7,6},{8,9},{9,8},{10,11... | collective-permute-start | bytes 4718600 | tf_op jit(solution)/shard_map/ppermute | solution.py:239
  71.4 3.4 %collective-permute-done.8.came_ref = f32[3,256,512]{2,1,0:T(8,128)S(1)} collective-permute-done((f32[3,256,512]{2,1,0:T(8,128)S(1)}, f32[3,256,512]{2,1,0:T(8,128)S(1)}, u32[]{:S(2)}, u32[]{:S(2)}) %collective-permute-start.8) | collective-permute-done | bytes 1572896 | tf_op jit(solution)/shard_map/ppermute | solution.py:239
  74.8 3.8 %shard_map.89 = bf16[256,3072]{1,0:T(8,128)(2,1)} custom-call(s32[2]{0:T(128)S(1)} %pad_add_fusion.at_ref, f32[3,256,512]{2,1,0:T(8,128)S(1)} %get-tuple-element.46.part_ref, f32[3,256,512]{2,1,0:T(8,128)S(1)} %collective-permute-done.8.came_ref, bf16[8,192,512]{2,1,0:T(8,128)(2,1)S(1)} %get-tuple-element.47.gate_w, ...), custom_call_target="tpu_custom_call" | custom-call | tf_op jit(solution)/shard_map/pallas_call | solution.py:188
  78.6 9.9 %all-to-all-start.1 = ((bf16[32,8,3072]{2,1,0:T(8,128)(2,1)}), bf16[32,8,3072]{2,1,0:T(8,128)(2,1)S(1)}, u32[]{:S(2)}, u32[]{:S(2)}) async-start(bf16[32,8,3072]{2,1,0:T(8,128)(2,1)} %bitcast.7), calls=%async_computation.1 | async-start | bytes 3145728 | tf_op jit(solution)/shard_map/all_to_all | solution.py:240
  88.5 0.1 copy.10.gates_ref
  88.6 0.1 copy.9.routes_ref
  88.7 39.4 %all-to-all-done.1 = bf16[32,8,3072]{2,1,0:T(8,128)(2,1)S(1)} async-done(((bf16[32,8,3072]{2,1,0:T(8,128)(2,1)}), bf16[32,8,3072]{2,1,0:T(8,128)(2,1)S(1)}, u32[]{:S(2)}, u32[]{:S(2)}) %all-to-all-start.1) | async-done | bytes 1572896 | tf_op jit(solution)/shard_map/all_to_all | solution.py:240
  128.1 0.8 shard_map.90
  129.0 12.7 %all_to_all.15 = bf16[8,16,384]{2,1,0:T(8,128)(2,1)S(1)} all-to-all(bf16[8,16,384]{2,1,0:T(8,128)(2,1)S(1)} %shard_map.90), channel_id=1, replica_groups=mesh['x'=4,'z'=8,'y'=8,'c'=2] {'y'}, dimensions={0} | all-to-all | bytes 196608 | tf_op jit(solution)/shard_map/all_to_all | solution.py:246
  141.7 0.7 fusion
  (19 shorter events, 0.1 us)
Async XLA Ops:
  3.8 61.4 %all-to-all-start = ((bf16[32,8,3072]{2,1,0:T(8,128)(2,1)}), bf16[32,8,3072]{2,1,0:T(8,128)(2,1)S(1)}, u32[]{:S(2)}, u32[]{:S(2)}) async-start(bf16[32,8,3072]{2,1,0:T(8,128)(2,1)} %bitcast.4), calls=%async_computation | async-start | bytes 3145728 | tf_op jit(solution)/shard_map/all_to_all | solution.py:215
  19.6 19.6 %collective-permute-start.4 = (bf16[2,1536,256]{2,1,0:T(8,128)(2,1)S(1)}, bf16[2,1536,256]{2,1,0:T(8,128)(2,1)S(1)}, u32[]{:S(2)}, u32[]{:S(2)}) collective-permute-start(bf16[2,1536,256]{2,1,0:T(8,128)(2,1)S(1)} %get-tuple-element.33), channel_id=1, source_target_pairs={{0,1},{1,0},{2,3},{3,2},{4,5},{5,4},{6,7},{7,6},{8,9},{9,8},{10,11... | collective-permute-start | bytes 4718600 | tf_op jit(solution)/shard_map/ppermute | solution.py:225
  21.6 23.7 %collective-permute-start = (bf16[192,512]{1,0:T(8,128)(2,1)S(1)}, bf16[192,512]{1,0:T(8,128)(2,1)S(1)}, u32[]{:S(2)}, u32[]{:S(2)}) collective-permute-start(bf16[192,512]{1,0:T(8,128)(2,1)S(1)} %get-tuple-element.26), channel_id=1, source_target_pairs={{0,8},{2,10},{4,12},{6,14},{8,0},{10,2},{12,4},{14,6},{1,9},{3,11}... | collective-permute-start | bytes 589832 | tf_op jit(solution)/shard_map/ppermute | solution.py:228
  28.4 23.3 %collective-permute-start.1 = (bf16[192,512]{1,0:T(8,128)(2,1)S(1)}, bf16[192,512]{1,0:T(8,128)(2,1)S(1)}, u32[]{:S(2)}, u32[]{:S(2)}) collective-permute-start(bf16[192,512]{1,0:T(8,128)(2,1)S(1)} %get-tuple-element.27), channel_id=1, source_target_pairs={{0,6},{2,8},{4,10},{6,12},{8,14},{10,0},{12,2},{14,4},{1,7},{3,9},... | collective-permute-start | bytes 589832 | tf_op jit(solution)/shard_map/ppermute | solution.py:228
  30.3 23.3 %collective-permute-start.2 = (bf16[192,512]{1,0:T(8,128)(2,1)S(1)}, bf16[192,512]{1,0:T(8,128)(2,1)S(1)}, u32[]{:S(2)}, u32[]{:S(2)}) collective-permute-start(bf16[192,512]{1,0:T(8,128)(2,1)S(1)} %get-tuple-element.28), channel_id=1, source_target_pairs={{0,10},{2,12},{4,14},{6,0},{8,2},{10,4},{12,6},{14,8},{1,11},{3,13... | collective-permute-start | bytes 589832 | tf_op jit(solution)/shard_map/ppermute | solution.py:228
  37.3 22.8 %collective-permute-start.3 = (bf16[192,512]{1,0:T(8,128)(2,1)S(1)}, bf16[192,512]{1,0:T(8,128)(2,1)S(1)}, u32[]{:S(2)}, u32[]{:S(2)}) collective-permute-start(bf16[192,512]{1,0:T(8,128)(2,1)S(1)} %get-tuple-element.29), channel_id=1, source_target_pairs={{0,4},{2,6},{4,8},{6,10},{8,12},{10,14},{12,0},{14,2},{1,5},{3,7},... | collective-permute-start | bytes 589832 | tf_op jit(solution)/shard_map/ppermute | solution.py:228
  39.2 26.0 %copy-start = (bf16[2,1536,256]{2,1,0:T(8,128)(2,1)}, bf16[2,1536,256]{2,1,0:T(8,128)(2,1)S(1)}, u32[]{:S(2)}) copy-start(bf16[2,1536,256]{2,1,0:T(8,128)(2,1)S(1)} %collective-permute-done.4.far_hbm) | copy-start | bytes 4718596
  39.2 20.9 %collective-permute-start.5 = (bf16[192,512]{1,0:T(8,128)(2,1)S(1)}, bf16[192,512]{1,0:T(8,128)(2,1)S(1)}, u32[]{:S(2)}, u32[]{:S(2)}) collective-permute-start(bf16[192,512]{1,0:T(8,128)(2,1)S(1)} %get-tuple-element.34), channel_id=1, source_target_pairs={{0,12},{2,14},{4,0},{6,2},{8,4},{10,6},{12,8},{14,10},{1,13},{3,15... | collective-permute-start | bytes 589832 | tf_op jit(solution)/shard_map/ppermute | solution.py:228
  45.3 20.0 %copy-start.1 = (bf16[192,512]{1,0:T(8,128)(2,1)}, bf16[192,512]{1,0:T(8,128)(2,1)S(1)}, u32[]{:S(2)}) copy-start(bf16[192,512]{1,0:T(8,128)(2,1)S(1)} %collective-permute-done.rest_0_) | copy-start | bytes 589828
  45.3 19.3 %collective-permute-start.6 = (bf16[192,512]{1,0:T(8,128)(2,1)S(1)}, bf16[192,512]{1,0:T(8,128)(2,1)S(1)}, u32[]{:S(2)}, u32[]{:S(2)}) collective-permute-start(bf16[192,512]{1,0:T(8,128)(2,1)S(1)} %get-tuple-element.35), channel_id=1, source_target_pairs={{0,2},{2,4},{4,6},{6,8},{8,10},{10,12},{12,14},{14,0},{1,3},{3,5},... | collective-permute-start | bytes 589832 | tf_op jit(solution)/shard_map/ppermute | solution.py:228
  51.7 13.6 %copy-start.2 = (bf16[192,512]{1,0:T(8,128)(2,1)}, bf16[192,512]{1,0:T(8,128)(2,1)S(1)}, u32[]{:S(2)}) copy-start(bf16[192,512]{1,0:T(8,128)(2,1)S(1)} %collective-permute-done.1.rest_1_) | copy-start | bytes 589828
  51.7 13.5 %collective-permute-start.7 = (bf16[192,512]{1,0:T(8,128)(2,1)S(1)}, bf16[192,512]{1,0:T(8,128)(2,1)}, u32[]{:S(2)}, u32[]{:S(2)}) collective-permute-start(bf16[192,512]{1,0:T(8,128)(2,1)S(1)} %get-tuple-element.36), channel_id=1, source_target_pairs={{0,14},{2,0},{4,2},{6,4},{8,6},{10,8},{12,10},{14,12},{1,15},{3,1}... | collective-permute-start | bytes 589832 | tf_op jit(solution)/shard_map/ppermute | solution.py:228
  53.7 10.9 %copy-start.3 = (bf16[192,512]{1,0:T(8,128)(2,1)}, bf16[192,512]{1,0:T(8,128)(2,1)S(1)}, u32[]{:S(2)}) copy-start(bf16[192,512]{1,0:T(8,128)(2,1)S(1)} %collective-permute-done.2.rest_2_) | copy-start | bytes 589828
  60.1 4.5 %copy-start.4 = (bf16[192,512]{1,0:T(8,128)(2,1)}, bf16[192,512]{1,0:T(8,128)(2,1)S(1)}, u32[]{:S(2)}) copy-start(bf16[192,512]{1,0:T(8,128)(2,1)S(1)} %collective-permute-done.3.rest_3_) | copy-start | bytes 589828
  60.1 4.5 %copy-start.5 = (bf16[192,512]{1,0:T(8,128)(2,1)}, bf16[192,512]{1,0:T(8,128)(2,1)S(1)}, u32[]{:S(2)}) copy-start(bf16[192,512]{1,0:T(8,128)(2,1)S(1)} %collective-permute-done.5.rest_4_) | copy-start | bytes 589828
  64.6 0.7 copy-start.6
  69.5 5.3 %collective-permute-start.8 = (f32[3,256,512]{2,1,0:T(8,128)S(1)}, f32[3,256,512]{2,1,0:T(8,128)S(1)}, u32[]{:S(2)}, u32[]{:S(2)}) collective-permute-start(f32[3,256,512]{2,1,0:T(8,128)S(1)} %get-tuple-element.46.part_ref), channel_id=1, source_target_pairs={{0,1},{1,0},{2,3},{3,2},{4,5},{5,4},{6,7},{7,6},{8,9},{9,8},{10,11... | collective-permute-start | bytes 4718600 | tf_op jit(solution)/shard_map/ppermute | solution.py:239
  78.6 9.9 %copy-start.7 = (f32[16,2]{0,1:T(2,128)S(1)}, f32[16,2]{0,1:T(2,128)}, u32[]{:S(2)}) copy-start(f32[16,2]{0,1:T(2,128)} %param.10) | copy-start | bytes 388
  78.6 10.0 %copy-start.8 = (s32[16,2]{0,1:T(2,128)S(1)}, s32[16,2]{0,1:T(2,128)}, u32[]{:S(2)}) copy-start(s32[16,2]{0,1:T(2,128)} %param.9) | copy-start | bytes 388
  78.6 49.5 %all-to-all-start.1 = ((bf16[32,8,3072]{2,1,0:T(8,128)(2,1)}), bf16[32,8,3072]{2,1,0:T(8,128)(2,1)S(1)}, u32[]{:S(2)}, u32[]{:S(2)}) async-start(bf16[32,8,3072]{2,1,0:T(8,128)(2,1)} %bitcast.7), calls=%async_computation.1 | async-start | bytes 3145728 | tf_op jit(solution)/shard_map/all_to_all | solution.py:240

commit v4 on v3

--- a/solution.py
+++ b/solution.py
@@ -100,45 +100,41 @@
         copy.wait()
 
 
-def weight_copies(at_ref, gate_hbm, up_hbm, far_hbm, down_hbm, pieces, gate_w, up_w, down_w, sems):
+def assemble_kernel(at_ref, gate_hbm, up_hbm, far_hbm, gate_w, up_w, sems):
     cols, width = gate_w.shape[1], gate_w.shape[2] // 2
-    steps = []
-    for i, shift in enumerate((0, *SHIFTS)):
+    moves = []
+    for i, (source, weight) in enumerate(((gate_hbm, gate_w), (up_hbm, up_w))):
+        for y in range(ROWS):
+            rows = pl.ds(pl.multiple_of((2 * y + at_ref[0]) * cols, cols), cols)
+            moves.append((source.at[rows], weight.at[y, :, pl.ds(0, width)]))
+            moves.append((far_hbm.at[i, pl.ds(y * cols, cols)], weight.at[y, :, pl.ds(width, width)]))
+    copies = [pltpu.make_async_copy(*move, sems.at[i]) for i, move in enumerate(moves)]
+    for copy in copies:
+        copy.start()
+    for copy in copies:
+        copy.wait()
+
+
+def before_kernel(at_ref, got_ref, gate_w, up_w, down_hbm, *rest):
+    pieces, (part_ref, down_w, sems) = rest[: ROWS - 1], rest[ROWS - 1 :]
+    width = part_ref.shape[2] // 2
+    half = got_ref.shape[1] // 2
+    own_units = pl.ds(pl.multiple_of(at_ref[1] * 2 * width, 2 * width), 2 * width)
+    copies = []
+    for i, (shift, piece) in enumerate(zip((0, *SHIFTS), (down_hbm.at[:, own_units], *pieces))):
         y = lax.rem(at_ref[1] - shift + ROWS, ROWS)
-        rows = pl.ds(pl.multiple_of((2 * y + at_ref[0]) * cols, cols), cols)
-        far = pl.ds(pl.multiple_of(y * cols, cols), cols)
-        own_units = pl.ds(pl.multiple_of(at_ref[1] * 2 * width, 2 * width), 2 * width)
-        moves = [
-            (gate_hbm.at[rows], gate_w.at[y, :, pl.ds(0, width)]),
-            (far_hbm.at[0, far], gate_w.at[y, :, pl.ds(width, width)]),
-            (up_hbm.at[rows], up_w.at[y, :, pl.ds(0, width)]),
-            (far_hbm.at[1, far], up_w.at[y, :, pl.ds(width, width)]),
-            (down_hbm.at[:, own_units] if shift == 0 else pieces[i - 1], down_w.at[y]),
-        ]
-        copies = [pltpu.make_async_copy(*move, sems.at[5 * i + j]) for j, move in enumerate(moves)]
-        steps.append((y, copies))
-    return steps
-
-
-def before_kernel(at_ref, got_ref, gate_hbm, up_hbm, far_hbm, down_hbm, *rest):
-    pieces, (part_ref, gate_w, up_w, down_w, sems) = rest[: ROWS - 1], rest[ROWS - 1 :]
-    steps = weight_copies(at_ref, gate_hbm, up_hbm, far_hbm, down_hbm, pieces, gate_w, up_w, down_w, sems)
-    for j in range(5):
-        for _, copies in steps:
-            copies[j].start()
+        copies.append(pltpu.make_async_copy(piece, down_w.at[y], sems.at[i]))
+    for copy in copies:
+        copy.start()
+    for i, weight in enumerate((gate_w, up_w)):
+        part_ref[i] = mm(got_ref[:, :half], weight[...].reshape(half, 2 * width))
+    for copy in copies:
+        copy.wait()
+    both = mm(got_ref[:, half:], down_w[...].reshape(half, 2 * width))
+    left, right = both[:, :width], both[:, width:]
     low = at_ref[0] == 0
-    half = got_ref.shape[1] // 2
-    width = part_ref.shape[2] // 2
-    for i, (weight, part, needs) in enumerate(((gate_w, 0, (0, 1)), (up_w, 0, (2, 3)), (down_w, 1, (4,)))):
-        for _, copies in steps:
-            for j in needs:
-                copies[j].wait()
-        both = mm(got_ref[:, part * half : (part + 1) * half], weight[...].reshape(half, 2 * width))
-        left, right = both[:, :width], both[:, width:]
-        if part:
-            left, right = jnp.where(low, left, right), jnp.where(low, right, left)
-        part_ref[i, :, :width] = left
-        part_ref[i, :, width:] = right
+    part_ref[2, :, :width] = jnp.where(low, left, right)
+    part_ref[2, :, width:] = jnp.where(low, right, left)
 
 
 def activations(gate_pre, up_pre, d_hidden):
@@ -153,17 +149,16 @@
 
 def after_kernel(at_ref, part_ref, came_ref, gate_w, up_w, down_w, sent_ref):
     low = at_ref[0] == 0
-    block = 2 * gate_w.shape[1]
     width = part_ref.shape[2] // 2
     own = activations(*(part_ref[i, :, :width] + came_ref[i, :, width:] for i in range(3)))
     far = activations(*(part_ref[i, :, width:] + came_ref[i, :, :width] for i in range(3)))
     hidden = jnp.concatenate([jnp.where(low, own[0], far[0]), jnp.where(low, far[0], own[0])], axis=1)
     d_gate = jnp.concatenate([own[1], far[1]], axis=1)
     d_up = jnp.concatenate([own[2], far[2]], axis=1)
-    for y in range(ROWS):
-        out = mm_t(hidden, down_w[y])
-        grad = mm_t(d_gate, gate_w[y]) + mm_t(d_up, up_w[y])
-        sent_ref[:, y * block : (y + 1) * block] = jnp.concatenate([out, grad], axis=1).astype(BF16)
+    half = sent_ref.shape[1] // 2
+    flat = lambda ref: ref[...].reshape(half, 2 * width)
+    sent_ref[:, :half] = mm_t(hidden, flat(down_w)).astype(BF16)
+    sent_ref[:, half:] = (mm_t(d_gate, flat(gate_w)) + mm_t(d_up, flat(up_w))).astype(BF16)
 
 
 def combine_kernel(back_ref, routes_ref, gates_ref, mixed_ref):
@@ -177,10 +172,11 @@
     def pick(weights, values):
         return jnp.dot(weights, values, precision=lax.Precision.HIGHEST, preferred_element_type=F32)
 
+    half = ROWS * cols
+    out, grad = pick(gate, summed[:, :half]), pick(mine, summed[:, half:])
     for y in range(ROWS):
-        out = pick(gate, summed[:, 2 * y * cols : (2 * y + 1) * cols])
-        grad = pick(mine, summed[:, (2 * y + 1) * cols : 2 * (y + 1) * cols])
-        mixed_ref[y] = jnp.concatenate([out, grad], axis=1).astype(BF16)
+        at = slice(y * cols, (y + 1) * cols)
+        mixed_ref[y] = jnp.concatenate([out[:, at], grad[:, at]], axis=1).astype(BF16)
 
 
 def call(kernel, out_shape, *args, scalars=0, mib=8):
@@ -227,15 +223,24 @@
     cut = (*cut[:4], *late)
     pieces = [lax.ppermute(a, "y", [(i, (i + s) % ROWS) for i in range(ROWS)]) for a, s in zip(cut, SHIFTS)]
 
-    got, *pieces = lax.optimization_barrier((got, *pieces))
-    part, *weights = pl.pallas_call(
+    gate_all, up_all = pl.pallas_call(
+        assemble_kernel,
+        in_specs=[SMEM] + [HBM] * 3,
+        out_specs=[VMEM] * 2,
+        out_shape=[pltpu.VMEM((ROWS, cols, 2 * width), BF16)] * 2,
+        scratch_shapes=[pltpu.SemaphoreType.DMA((4 * ROWS,))],
+        compiler_params=params(1),
+    )(at, pin(w_gate), pin(w_up), far)
+    got, gate_all, up_all, *pieces = lax.optimization_barrier((got, gate_all, up_all, *pieces))
+    part, down_all = pl.pallas_call(
         before_kernel,
-        in_specs=[SMEM, VMEM] + [HBM] * (3 + ROWS),
-        out_specs=[VMEM] * 4,
-        out_shape=[shape(3, lines, 2 * width, dtype=F32)] + [shape(ROWS, cols, 2 * width)] * 3,
-        scratch_shapes=[pltpu.SemaphoreType.DMA((5 * ROWS,))],
-        compiler_params=params(8),
-    )(at, got.reshape(lines, model), *(pin(a) for a in (w_gate, w_up, far, down, *pieces)))
+        in_specs=[SMEM] + [VMEM] * 3 + [HBM] * ROWS,
+        out_specs=[VMEM] * 2,
+        out_shape=[shape(3, lines, 2 * width, dtype=F32), shape(ROWS, cols, 2 * width)],
+        scratch_shapes=[pltpu.SemaphoreType.DMA((ROWS,))],
+        compiler_params=params(4),
+    )(at, got.reshape(lines, model), gate_all, up_all, *(pin(a) for a in (down, *pieces)))
+    weights = (gate_all, up_all, down_all)
     sent = call(after_kernel, shape(lines, model), at, part, lax.ppermute(part, "c", SWAP), *weights, scalars=1)
     back = lax.all_to_all(sent.reshape(n_dp, CAP, model), DP, split_axis=0, concat_axis=0, tiled=True)
     mixed = call(

time: 143 us -> 143 us (level)
  waiting for transfers between devices: 58.2 us -> 55.9 us
  Pallas kernels: 14.6 us -> 16.3 us
    pallas_call x1 -> x2, Pallas kernels: 4.18 us -> 6.59 us  [the longest x1 4.28 us: body(): pl.pallas_call(before_kernel, in_specs=[SMEM] + [VMEM] * 3 + [HBM] * ROWS...]
    ppermute x7, waiting for transfers between devices: 15.4 us -> 13 us  [body(): lax.ppermute(a, 'y', [(i, (i + s) % ROWS) for i in range(ROWS)])]
  transfers between devices with their start and end apart: 11 -> 11, of which waited for: 5 -> 5; matrix products, arithmetic and copies ran while one was open for 0% -> 0% of each run, Pallas kernels for 2% -> 3%
where the time goes in v4:
time: 143 us; the launch traced here: 142 us
  waiting for transfers between devices  55.9 us (39%)
  starting transfers between devices  54.5 us (38%)
  Pallas kernels  16.3 us (11%)
  blocking collectives  12.7 us (9%)
  local copies, waits for them, and re-layouts  1.55 us (1%)
    all_to_all x2, waiting for transfers between devices, body(): lax.all_to_all(sent.reshape(n_dp, CAP, model), DP, split_axis=0, concat_a...  39.4 us
    ppermute x7, starting transfers between devices, body(): lax.ppermute(a, 'y', [(i, (i + s) % ROWS) for i in range(ROWS)])  27.5 us
    all_to_all x2, starting transfers between devices, body(): lax.all_to_all(sent.reshape(n_dp, CAP, model), DP, split_axis=0, concat_a...  23.1 us
    ppermute x7, waiting for transfers between devices, body(): lax.ppermute(a, 'y', [(i, (i + s) % ROWS) for i in range(ROWS)])  13 us
    all_to_all x1, blocking collectives, body(): mixed = lax.all_to_all(mixed, 'y', split_axis=0, concat_axis=0, tiled=True)  12.7 us
    pallas_call x1, Pallas kernels, body(): pl.pallas_call(before_kernel, in_specs=[SMEM] + [VMEM] * 3 + [HBM] * ROWS...  4.28 us
    pallas_call x2, Pallas kernels, call(): pl.pallas_call(kernel, in_specs=[SMEM] * scalars + [VMEM] * (len(args) -...  3.98 us
    ppermute x1, waiting for transfers between devices, body(): lax.ppermute(part, 'c', SWAP)  3.38 us
  transfers between devices with their start and end apart: 11, of which 5 were waited for; matrix products, arithmetic and copies ran while one was open for 0% of the time, Pallas kernels for 3%

profile of v4, /device:TPU:8, one launch (start us, length us, event | category | flops | bytes accessed | tf_op | source)
XLA Modules:
  0.0 141.8 jit_solution(5625731867324432589)
XLA Ops:
  0.6 0.1 pad_add_fusion.at_ref
  0.7 3.1 %shard_map.86 = bf16[8,4,8,3072]{3,2,1,0:T(8,128)(2,1)} custom-call(s32[2]{0:T(128)S(1)} %pad_add_fusion.at_ref, bf16[16,3072]{1,0:T(8,128)(2,1)} %tokens_hbm.1, bf16[16,3072]{1,0:T(8,128)(2,1)} %cot_hbm.1, s32[2,16]{1,0:T(2,128)} %bitcast.13, f32[2,16]{1,0:T(2,128)} %bitcast.12), custom_call_target="tpu_custom_call" | custom-call | tf_op jit(solution)/shard_map/pallas_call | solution.py:203
  3.8 13.3 %all-to-all-start = ((bf16[32,8,3072]{2,1,0:T(8,128)(2,1)}), bf16[32,8,3072]{2,1,0:T(8,128)(2,1)}, u32[]{:S(2)}, u32[]{:S(2)}) async-start(bf16[32,8,3072]{2,1,0:T(8,128)(2,1)} %bitcast.4), calls=%async_computation | async-start | bytes 3145728 | tf_op jit(solution)/shard_map/all_to_all | solution.py:211
  17.1 2.6 %shard_map.87 = (bf16[192,512]{1,0:T(8,128)(2,1)S(1)}, bf16[192,512]{1,0:T(8,128)(2,1)S(1)}, bf16[192,512]{1,0:T(8,128)(2,1)S(1)}, bf16[192,512]{1,0:T(8,128)(2,...) custom-call(s32[2]{0:T(128)S(1)} %pad_add_fusion.at_ref, ...), custom_call_target="tpu_custom_call" | custom-call | tf_op jit(solution)/shard_map/pallas_call | solution.py:213
  19.7 1.9 %collective-permute-start = (bf16[2,1536,256]{2,1,0:T(8,128)(2,1)S(1)}, bf16[2,1536,256]{2,1,0:T(8,128)(2,1)S(1)}, u32[]{:S(2)}, u32[]{:S(2)}) collective-permute-start(bf16[2,1536,256]{2,1,0:T(8,128)(2,1)S(1)} %get-tuple-element.31), channel_id=1, source_target_pairs={{0,1},{1,0},{2,3},{3,2},{4,5},{5,4},{6,7},{7,6},{8,9},{9,8},{10,11... | collective-permute-start | bytes 4718600 | tf_op jit(solution)/shard_map/ppermute | solution.py:221
  21.7 6.8 %collective-permute-start.1 = (bf16[192,512]{1,0:T(8,128)(2,1)S(1)}, bf16[192,512]{1,0:T(8,128)(2,1)S(1)}, u32[]{:S(2)}, u32[]{:S(2)}) collective-permute-start(bf16[192,512]{1,0:T(8,128)(2,1)S(1)} %get-tuple-element.35), channel_id=1, source_target_pairs={{0,8},{2,10},{4,12},{6,14},{8,0},{10,2},{12,4},{14,6},{1,9},{3,11}... | collective-permute-start | bytes 589832 | tf_op jit(solution)/shard_map/ppermute | solution.py:224
  28.5 1.9 %collective-permute-start.2 = (bf16[192,512]{1,0:T(8,128)(2,1)S(1)}, bf16[192,512]{1,0:T(8,128)(2,1)S(1)}, u32[]{:S(2)}, u32[]{:S(2)}) collective-permute-start(bf16[192,512]{1,0:T(8,128)(2,1)S(1)} %get-tuple-element.36), channel_id=1, source_target_pairs={{0,6},{2,8},{4,10},{6,12},{8,14},{10,0},{12,2},{14,4},{1,7},{3,9},... | collective-permute-start | bytes 589832 | tf_op jit(solution)/shard_map/ppermute | solution.py:224
  30.4 6.9 %collective-permute-start.3 = (bf16[192,512]{1,0:T(8,128)(2,1)S(1)}, bf16[192,512]{1,0:T(8,128)(2,1)S(1)}, u32[]{:S(2)}, u32[]{:S(2)}) collective-permute-start(bf16[192,512]{1,0:T(8,128)(2,1)S(1)} %get-tuple-element.37), channel_id=1, source_target_pairs={{0,10},{2,12},{4,14},{6,0},{8,2},{10,4},{12,6},{14,8},{1,11},{3,13... | collective-permute-start | bytes 589832 | tf_op jit(solution)/shard_map/ppermute | solution.py:224
  37.4 1.9 %collective-permute-start.4 = (bf16[192,512]{1,0:T(8,128)(2,1)S(1)}, bf16[192,512]{1,0:T(8,128)(2,1)S(1)}, u32[]{:S(2)}, u32[]{:S(2)}) collective-permute-start(bf16[192,512]{1,0:T(8,128)(2,1)S(1)} %get-tuple-element.38), channel_id=1, source_target_pairs={{0,4},{2,6},{4,8},{6,10},{8,12},{10,14},{12,0},{14,2},{1,5},{3,7},... | collective-permute-start | bytes 589832 | tf_op jit(solution)/shard_map/ppermute | solution.py:224
  39.3 0.0 collective-permute-done.far_hbm
  39.3 6.0 %collective-permute-start.5 = (bf16[192,512]{1,0:T(8,128)(2,1)S(1)}, bf16[192,512]{1,0:T(8,128)(2,1)S(1)}, u32[]{:S(2)}, u32[]{:S(2)}) collective-permute-start(bf16[192,512]{1,0:T(8,128)(2,1)S(1)} %get-tuple-element.39), channel_id=1, source_target_pairs={{0,12},{2,14},{4,0},{6,2},{8,4},{10,6},{12,8},{14,10},{1,13},{3,15... | collective-permute-start | bytes 589832 | tf_op jit(solution)/shard_map/ppermute | solution.py:224
  45.3 0.0 collective-permute-done.1.rest_0_
  45.4 1.9 %collective-permute-start.6 = (bf16[192,512]{1,0:T(8,128)(2,1)S(1)}, bf16[192,512]{1,0:T(8,128)(2,1)S(1)}, u32[]{:S(2)}, u32[]{:S(2)}) collective-permute-start(bf16[192,512]{1,0:T(8,128)(2,1)S(1)} %get-tuple-element.40), channel_id=1, source_target_pairs={{0,2},{2,4},{4,6},{6,8},{8,10},{10,12},{12,14},{14,0},{1,3},{3,5},... | collective-permute-start | bytes 589832 | tf_op jit(solution)/shard_map/ppermute | solution.py:224
  47.3 4.5 %collective-permute-done.2.rest_1_ = bf16[192,512]{1,0:T(8,128)(2,1)S(1)} collective-permute-done((bf16[192,512]{1,0:T(8,128)(2,1)S(1)}, bf16[192,512]{1,0:T(8,128)(2,1)S(1)}, u32[]{:S(2)}, u32[]{:S(2)}) %collective-permute-start.2) | collective-permute-done | bytes 196640 | tf_op jit(solution)/shard_map/ppermute | solution.py:224
  51.8 1.9 %collective-permute-start.7 = (bf16[192,512]{1,0:T(8,128)(2,1)S(1)}, bf16[192,512]{1,0:T(8,128)(2,1)}, u32[]{:S(2)}, u32[]{:S(2)}) collective-permute-start(bf16[192,512]{1,0:T(8,128)(2,1)S(1)} %get-tuple-element.41), channel_id=1, source_target_pairs={{0,14},{2,0},{4,2},{6,4},{8,6},{10,8},{12,10},{14,12},{1,15},{3,1}... | collective-permute-start | bytes 589832 | tf_op jit(solution)/shard_map/ppermute | solution.py:224
  53.7 2.3 %shard_map.88 = (bf16[8,192,512]{2,1,0:T(8,128)(2,1)S(1)}, bf16[8,192,512]{2,1,0:T(8,128)(2,1)S(1)}) custom-call(s32[2]{0:T(128)S(1)} %pad_add_fusion.at_ref, bf16[3072,256]{1,0:T(8,128)(2,1)} %gate_hbm.3, bf16[3072,256]{1,0:T(8,128)(2,1)} %up_hbm.3, bf16[2,1536,256]{2,1,0:T(8,128)(2,1)S(1)} %collective-permute-done.far_hbm), custom_call_target="tpu_custom_call" | custom-call | tf_op jit(solution)/shard_map/pallas_call | solution.py:226
  56.1 4.1 %collective-permute-done.4.rest_3_ = bf16[192,512]{1,0:T(8,128)(2,1)S(1)} collective-permute-done((bf16[192,512]{1,0:T(8,128)(2,1)S(1)}, bf16[192,512]{1,0:T(8,128)(2,1)S(1)}, u32[]{:S(2)}, u32[]{:S(2)}) %collective-permute-start.4) | collective-permute-done | bytes 196640 | tf_op jit(solution)/shard_map/ppermute | solution.py:224
  60.2 4.4 %collective-permute-done.6.rest_5_ = bf16[192,512]{1,0:T(8,128)(2,1)S(1)} collective-permute-done((bf16[192,512]{1,0:T(8,128)(2,1)S(1)}, bf16[192,512]{1,0:T(8,128)(2,1)S(1)}, u32[]{:S(2)}, u32[]{:S(2)}) %collective-permute-start.6) | collective-permute-done | bytes 196640 | tf_op jit(solution)/shard_map/ppermute | solution.py:224
  64.7 0.7 copy-done.5
  65.3 0.0 collective-permute-done.7.rest_6_
  65.3 0.0 all-to-all-done
  65.3 4.3 %shard_map.89 = (f32[3,256,512]{2,1,0:T(8,128)S(1)}, bf16[8,192,512]{2,1,0:T(8,128)(2,1)S(1)}) custom-call(s32[2]{0:T(128)S(1)} %pad_add_fusion.at_ref, bf16[256,3072]{1,0:T(8,128)(2,1)} %bitcast.6.got_ref, bf16[8,192,512]{2,1,0:T(8,128)(2,1)S(1)} %get-tuple-element.43.gate_w, bf16[8,192,512]{2,1,0:T(8,128)(2,1)S(1)} %get-tuple-element.44.up_w, ...), custom_call_target="tpu_custom_call" | custom-call | tf_op jit(solution)/shard_map/pallas_call | solution.py:235
  69.6 1.9 %collective-permute-start.8 = (f32[3,256,512]{2,1,0:T(8,128)S(1)}, f32[3,256,512]{2,1,0:T(8,128)S(1)}, u32[]{:S(2)}, u32[]{:S(2)}) collective-permute-start(f32[3,256,512]{2,1,0:T(8,128)S(1)} %get-tuple-element.52.part_ref), channel_id=1, source_target_pairs={{0,1},{1,0},{2,3},{3,2},{4,5},{5,4},{6,7},{7,6},{8,9},{9,8},{10,11... | collective-permute-start | bytes 4718600 | tf_op jit(solution)/shard_map/ppermute | solution.py:244
  71.5 3.4 %collective-permute-done.8.came_ref = f32[3,256,512]{2,1,0:T(8,128)S(1)} collective-permute-done((f32[3,256,512]{2,1,0:T(8,128)S(1)}, f32[3,256,512]{2,1,0:T(8,128)S(1)}, u32[]{:S(2)}, u32[]{:S(2)}) %collective-permute-start.8) | collective-permute-done | bytes 1572896 | tf_op jit(solution)/shard_map/ppermute | solution.py:244
  74.9 3.3 %shard_map.90 = bf16[256,3072]{1,0:T(8,128)(2,1)} custom-call(s32[2]{0:T(128)S(1)} %pad_add_fusion.at_ref, f32[3,256,512]{2,1,0:T(8,128)S(1)} %get-tuple-element.52.part_ref, f32[3,256,512]{2,1,0:T(8,128)S(1)} %collective-permute-done.8.came_ref, bf16[8,192,512]{2,1,0:T(8,128)(2,1)S(1)} %get-tuple-element.43.gate_w, ...), custom_call_target="tpu_custom_call" | custom-call | tf_op jit(solution)/shard_map/pallas_call | solution.py:184
  78.2 9.9 %all-to-all-start.1 = ((bf16[32,8,3072]{2,1,0:T(8,128)(2,1)}), bf16[32,8,3072]{2,1,0:T(8,128)(2,1)S(1)}, u32[]{:S(2)}, u32[]{:S(2)}) async-start(bf16[32,8,3072]{2,1,0:T(8,128)(2,1)} %bitcast.7), calls=%async_computation.1 | async-start | bytes 3145728 | tf_op jit(solution)/shard_map/all_to_all | solution.py:245
  88.1 0.1 copy.10.gates_ref
  88.1 0.1 copy.9.routes_ref
  88.2 39.4 %all-to-all-done.1 = bf16[32,8,3072]{2,1,0:T(8,128)(2,1)S(1)} async-done(((bf16[32,8,3072]{2,1,0:T(8,128)(2,1)}), bf16[32,8,3072]{2,1,0:T(8,128)(2,1)S(1)}, u32[]{:S(2)}, u32[]{:S(2)}) %all-to-all-start.1) | async-done | bytes 1572896 | tf_op jit(solution)/shard_map/all_to_all | solution.py:245
  127.7 0.7 shard_map.91
  128.4 12.7 %all_to_all.15 = bf16[8,16,384]{2,1,0:T(8,128)(2,1)S(1)} all-to-all(bf16[8,16,384]{2,1,0:T(8,128)(2,1)S(1)} %shard_map.91), channel_id=1, replica_groups=mesh['x'=4,'z'=8,'y'=8,'c'=2] {'y'}, dimensions={0} | all-to-all | bytes 196608 | tf_op jit(solution)/shard_map/all_to_all | solution.py:251
  141.1 0.7 fusion
  (18 shorter events, 0.1 us)
Async XLA Ops:
  3.8 61.6 %all-to-all-start = ((bf16[32,8,3072]{2,1,0:T(8,128)(2,1)}), bf16[32,8,3072]{2,1,0:T(8,128)(2,1)}, u32[]{:S(2)}, u32[]{:S(2)}) async-start(bf16[32,8,3072]{2,1,0:T(8,128)(2,1)} %bitcast.4), calls=%async_computation | async-start | bytes 3145728 | tf_op jit(solution)/shard_map/all_to_all | solution.py:211
  19.7 19.6 %collective-permute-start = (bf16[2,1536,256]{2,1,0:T(8,128)(2,1)S(1)}, bf16[2,1536,256]{2,1,0:T(8,128)(2,1)S(1)}, u32[]{:S(2)}, u32[]{:S(2)}) collective-permute-start(bf16[2,1536,256]{2,1,0:T(8,128)(2,1)S(1)} %get-tuple-element.31), channel_id=1, source_target_pairs={{0,1},{1,0},{2,3},{3,2},{4,5},{5,4},{6,7},{7,6},{8,9},{9,8},{10,11... | collective-permute-start | bytes 4718600 | tf_op jit(solution)/shard_map/ppermute | solution.py:221
  21.7 23.7 %collective-permute-start.1 = (bf16[192,512]{1,0:T(8,128)(2,1)S(1)}, bf16[192,512]{1,0:T(8,128)(2,1)S(1)}, u32[]{:S(2)}, u32[]{:S(2)}) collective-permute-start(bf16[192,512]{1,0:T(8,128)(2,1)S(1)} %get-tuple-element.35), channel_id=1, source_target_pairs={{0,8},{2,10},{4,12},{6,14},{8,0},{10,2},{12,4},{14,6},{1,9},{3,11}... | collective-permute-start | bytes 589832 | tf_op jit(solution)/shard_map/ppermute | solution.py:224
  28.5 23.3 %collective-permute-start.2 = (bf16[192,512]{1,0:T(8,128)(2,1)S(1)}, bf16[192,512]{1,0:T(8,128)(2,1)S(1)}, u32[]{:S(2)}, u32[]{:S(2)}) collective-permute-start(bf16[192,512]{1,0:T(8,128)(2,1)S(1)} %get-tuple-element.36), channel_id=1, source_target_pairs={{0,6},{2,8},{4,10},{6,12},{8,14},{10,0},{12,2},{14,4},{1,7},{3,9},... | collective-permute-start | bytes 589832 | tf_op jit(solution)/shard_map/ppermute | solution.py:224
  30.4 25.7 %collective-permute-start.3 = (bf16[192,512]{1,0:T(8,128)(2,1)S(1)}, bf16[192,512]{1,0:T(8,128)(2,1)S(1)}, u32[]{:S(2)}, u32[]{:S(2)}) collective-permute-start(bf16[192,512]{1,0:T(8,128)(2,1)S(1)} %get-tuple-element.37), channel_id=1, source_target_pairs={{0,10},{2,12},{4,14},{6,0},{8,2},{10,4},{12,6},{14,8},{1,11},{3,13... | collective-permute-start | bytes 589832 | tf_op jit(solution)/shard_map/ppermute | solution.py:224
  37.4 22.8 %collective-permute-start.4 = (bf16[192,512]{1,0:T(8,128)(2,1)S(1)}, bf16[192,512]{1,0:T(8,128)(2,1)S(1)}, u32[]{:S(2)}, u32[]{:S(2)}) collective-permute-start(bf16[192,512]{1,0:T(8,128)(2,1)S(1)} %get-tuple-element.38), channel_id=1, source_target_pairs={{0,4},{2,6},{4,8},{6,10},{8,12},{10,14},{12,0},{14,2},{1,5},{3,7},... | collective-permute-start | bytes 589832 | tf_op jit(solution)/shard_map/ppermute | solution.py:224
  39.3 20.9 %collective-permute-start.5 = (bf16[192,512]{1,0:T(8,128)(2,1)S(1)}, bf16[192,512]{1,0:T(8,128)(2,1)S(1)}, u32[]{:S(2)}, u32[]{:S(2)}) collective-permute-start(bf16[192,512]{1,0:T(8,128)(2,1)S(1)} %get-tuple-element.39), channel_id=1, source_target_pairs={{0,12},{2,14},{4,0},{6,2},{8,4},{10,6},{12,8},{14,10},{1,13},{3,15... | collective-permute-start | bytes 589832 | tf_op jit(solution)/shard_map/ppermute | solution.py:224
  45.4 10.7 %copy-start = (bf16[192,512]{1,0:T(8,128)(2,1)}, bf16[192,512]{1,0:T(8,128)(2,1)S(1)}, u32[]{:S(2)}) copy-start(bf16[192,512]{1,0:T(8,128)(2,1)S(1)} %collective-permute-done.1.rest_0_) | copy-start | bytes 589828
  45.4 19.3 %collective-permute-start.6 = (bf16[192,512]{1,0:T(8,128)(2,1)S(1)}, bf16[192,512]{1,0:T(8,128)(2,1)S(1)}, u32[]{:S(2)}, u32[]{:S(2)}) collective-permute-start(bf16[192,512]{1,0:T(8,128)(2,1)S(1)} %get-tuple-element.40), channel_id=1, source_target_pairs={{0,2},{2,4},{4,6},{6,8},{8,10},{10,12},{12,14},{14,0},{1,3},{3,5},... | collective-permute-start | bytes 589832 | tf_op jit(solution)/shard_map/ppermute | solution.py:224
  51.8 4.3 %copy-start.1 = (bf16[192,512]{1,0:T(8,128)(2,1)}, bf16[192,512]{1,0:T(8,128)(2,1)S(1)}, u32[]{:S(2)}) copy-start(bf16[192,512]{1,0:T(8,128)(2,1)S(1)} %collective-permute-done.2.rest_1_) | copy-start | bytes 589828
  51.8 13.5 %collective-permute-start.7 = (bf16[192,512]{1,0:T(8,128)(2,1)S(1)}, bf16[192,512]{1,0:T(8,128)(2,1)}, u32[]{:S(2)}, u32[]{:S(2)}) collective-permute-start(bf16[192,512]{1,0:T(8,128)(2,1)S(1)} %get-tuple-element.41), channel_id=1, source_target_pairs={{0,14},{2,0},{4,2},{6,4},{8,6},{10,8},{12,10},{14,12},{1,15},{3,1}... | collective-permute-start | bytes 589832 | tf_op jit(solution)/shard_map/ppermute | solution.py:224
  56.1 8.6 %copy-start.2 = (bf16[192,512]{1,0:T(8,128)(2,1)}, bf16[192,512]{1,0:T(8,128)(2,1)S(1)}, u32[]{:S(2)}) copy-start(bf16[192,512]{1,0:T(8,128)(2,1)S(1)} %collective-permute-done.3.rest_2_) | copy-start | bytes 589828
  60.2 4.5 %copy-start.3 = (bf16[192,512]{1,0:T(8,128)(2,1)}, bf16[192,512]{1,0:T(8,128)(2,1)S(1)}, u32[]{:S(2)}) copy-start(bf16[192,512]{1,0:T(8,128)(2,1)S(1)} %collective-permute-done.4.rest_3_) | copy-start | bytes 589828
  60.2 4.5 %copy-start.4 = (bf16[192,512]{1,0:T(8,128)(2,1)}, bf16[192,512]{1,0:T(8,128)(2,1)S(1)}, u32[]{:S(2)}) copy-start(bf16[192,512]{1,0:T(8,128)(2,1)S(1)} %collective-permute-done.5.rest_4_) | copy-start | bytes 589828
  64.6 0.7 copy-start.5
  69.6 5.3 %collective-permute-start.8 = (f32[3,256,512]{2,1,0:T(8,128)S(1)}, f32[3,256,512]{2,1,0:T(8,128)S(1)}, u32[]{:S(2)}, u32[]{:S(2)}) collective-permute-start(f32[3,256,512]{2,1,0:T(8,128)S(1)} %get-tuple-element.52.part_ref), channel_id=1, source_target_pairs={{0,1},{1,0},{2,3},{3,2},{4,5},{5,4},{6,7},{7,6},{8,9},{9,8},{10,11... | collective-permute-start | bytes 4718600 | tf_op jit(solution)/shard_map/ppermute | solution.py:244
  78.2 9.9 %copy-start.6 = (f32[16,2]{0,1:T(2,128)S(1)}, f32[16,2]{0,1:T(2,128)}, u32[]{:S(2)}) copy-start(f32[16,2]{0,1:T(2,128)} %param.10) | copy-start | bytes 388
  78.2 10.0 %copy-start.7 = (s32[16,2]{0,1:T(2,128)S(1)}, s32[16,2]{0,1:T(2,128)}, u32[]{:S(2)}) copy-start(s32[16,2]{0,1:T(2,128)} %param.9) | copy-start | bytes 388
  78.2 49.5 %all-to-all-start.1 = ((bf16[32,8,3072]{2,1,0:T(8,128)(2,1)}), bf16[32,8,3072]{2,1,0:T(8,128)(2,1)S(1)}, u32[]{:S(2)}, u32[]{:S(2)}) async-start(bf16[32,8,3072]{2,1,0:T(8,128)(2,1)} %bitcast.7), calls=%async_computation.1 | async-start | bytes 3145728 | tf_op jit(solution)/shard_map/all_to_all | solution.py:245

commit v5 on v4

--- a/solution.py
+++ b/solution.py
@@ -115,20 +115,26 @@
         copy.wait()
 
 
-def before_kernel(at_ref, got_ref, gate_w, up_w, down_hbm, *rest):
-    pieces, (part_ref, down_w, sems) = rest[: ROWS - 1], rest[ROWS - 1 :]
+def before_kernel(at_ref, got_hbm, gate_w, up_w, down_hbm, *rest):
+    pieces, (part_ref, down_w, got_ref, sems) = rest[: ROWS - 1], rest[ROWS - 1 :]
     width = part_ref.shape[2] // 2
     half = got_ref.shape[1] // 2
     own_units = pl.ds(pl.multiple_of(at_ref[1] * 2 * width, 2 * width), 2 * width)
+    halves = []
+    for i in range(2):
+        at = pl.ds(i * half, half)
+        halves.append(pltpu.make_async_copy(got_hbm.at[:, at], got_ref.at[:, at], sems.at[ROWS + i]))
+        halves[i].start()
     copies = []
     for i, (shift, piece) in enumerate(zip((0, *SHIFTS), (down_hbm.at[:, own_units], *pieces))):
         y = lax.rem(at_ref[1] - shift + ROWS, ROWS)
         copies.append(pltpu.make_async_copy(piece, down_w.at[y], sems.at[i]))
     for copy in copies:
         copy.start()
+    halves[0].wait()
     for i, weight in enumerate((gate_w, up_w)):
         part_ref[i] = mm(got_ref[:, :half], weight[...].reshape(half, 2 * width))
-    for copy in copies:
+    for copy in (halves[1], *copies):
         copy.wait()
     both = mm(got_ref[:, half:], down_w[...].reshape(half, 2 * width))
     left, right = both[:, :width], both[:, width:]
@@ -147,7 +153,7 @@
     )
 
 
-def after_kernel(at_ref, part_ref, came_ref, gate_w, up_w, down_w, sent_ref):
+def after_kernel(at_ref, part_ref, came_ref, gate_w, up_w, down_w, sent_hbm, held, sems):
     low = at_ref[0] == 0
     width = part_ref.shape[2] // 2
     own = activations(*(part_ref[i, :, :width] + came_ref[i, :, width:] for i in range(3)))
@@ -155,10 +161,20 @@
     hidden = jnp.concatenate([jnp.where(low, own[0], far[0]), jnp.where(low, far[0], own[0])], axis=1)
     d_gate = jnp.concatenate([own[1], far[1]], axis=1)
     d_up = jnp.concatenate([own[2], far[2]], axis=1)
-    half = sent_ref.shape[1] // 2
+    half = held.shape[1] // 2
     flat = lambda ref: ref[...].reshape(half, 2 * width)
-    sent_ref[:, :half] = mm_t(hidden, flat(down_w)).astype(BF16)
-    sent_ref[:, half:] = (mm_t(d_gate, flat(gate_w)) + mm_t(d_up, flat(up_w))).astype(BF16)
+    copies = []
+    for i in range(2):
+        part = pl.ds(i * half, half)
+        if i == 0:
+            values = mm_t(hidden, flat(down_w))
+        else:
+            values = mm_t(d_gate, flat(gate_w)) + mm_t(d_up, flat(up_w))
+        held[:, part] = values.astype(BF16)
+        copies.append(pltpu.make_async_copy(held.at[:, part], sent_hbm.at[:, part], sems.at[i]))
+        copies[i].start()
+    for copy in copies:
+        copy.wait()
 
 
 def combine_kernel(back_ref, routes_ref, gates_ref, mixed_ref):
@@ -234,14 +250,21 @@
     got, gate_all, up_all, *pieces = lax.optimization_barrier((got, gate_all, up_all, *pieces))
     part, down_all = pl.pallas_call(
         before_kernel,
-        in_specs=[SMEM] + [VMEM] * 3 + [HBM] * ROWS,
+        in_specs=[SMEM, HBM] + [VMEM] * 2 + [HBM] * ROWS,
         out_specs=[VMEM] * 2,
         out_shape=[shape(3, lines, 2 * width, dtype=F32), shape(ROWS, cols, 2 * width)],
-        scratch_shapes=[pltpu.SemaphoreType.DMA((ROWS,))],
-        compiler_params=params(4),
-    )(at, got.reshape(lines, model), gate_all, up_all, *(pin(a) for a in (down, *pieces)))
+        scratch_shapes=[pltpu.VMEM((lines, model), BF16), pltpu.SemaphoreType.DMA((ROWS + 2,))],
+        compiler_params=params(6),
+    )(at, pin(got.reshape(lines, model)), gate_all, up_all, *(pin(a) for a in (down, *pieces)))
     weights = (gate_all, up_all, down_all)
-    sent = call(after_kernel, shape(lines, model), at, part, lax.ppermute(part, "c", SWAP), *weights, scalars=1)
+    sent = pl.pallas_call(
+        after_kernel,
+        in_specs=[SMEM] + [VMEM] * 5,
+        out_specs=HBM,
+        out_shape=shape(lines, model),
+        scratch_shapes=[pltpu.VMEM((lines, model), BF16), pltpu.SemaphoreType.DMA((2,))],
+        compiler_params=params(10),
+    )(at, part, lax.ppermute(part, "c", SWAP), *weights)
     back = lax.all_to_all(sent.reshape(n_dp, CAP, model), DP, split_axis=0, concat_axis=0, tiled=True)
     mixed = call(
         combine_kernel,

time: 143 us -> 141 us (0.986)
    pallas_call x2 -> x1, Pallas kernels: 3.98 us -> 0.72 us  [call(): pl.pallas_call(kernel, in_specs=[SMEM] * scalars + [VMEM] * (len(args) -...]
    pallas_call x1 -> x2, Pallas kernels: 4.28 us -> 6.36 us  [the longest x1 3.34 us: body(): pl.pallas_call(before_kernel, in_specs=[SMEM, HBM] + [VMEM] * 2 + [HBM] *...]
  transfers between devices with their start and end apart: 11 -> 11, of which waited for: 5 -> 5; matrix products, arithmetic and copies ran while one was open for 0% -> 0% of each run, Pallas kernels for 3% -> 4%
where the time goes in v5:
time: 141 us
  waiting for transfers between devices  55.8 us (40%)
  starting transfers between devices  54.4 us (39%)
  Pallas kernels  15.1 us (11%)
  blocking collectives  12.7 us (9%)
  local copies, waits for them, and re-layouts  1.55 us (1%)
    all_to_all x2, waiting for transfers between devices, body(): lax.all_to_all(sent.reshape(n_dp, CAP, model), DP, split_axis=0, concat_a...  39.4 us
    ppermute x7, starting transfers between devices, body(): lax.ppermute(a, 'y', [(i, (i + s) % ROWS) for i in range(ROWS)])  27.5 us
    all_to_all x2, starting transfers between devices, body(): lax.all_to_all(sent.reshape(n_dp, CAP, model), DP, split_axis=0, concat_a...  23 us
    ppermute x7, waiting for transfers between devices, body(): lax.ppermute(a, 'y', [(i, (i + s) % ROWS) for i in range(ROWS)])  13 us
    all_to_all x1, blocking collectives, body(): mixed = lax.all_to_all(mixed, 'y', split_axis=0, concat_axis=0, tiled=True)  12.7 us
    ppermute x1, waiting for transfers between devices, body(): lax.ppermute(part, 'c', SWAP)  3.38 us
    pallas_call x1, Pallas kernels, body(): pl.pallas_call(before_kernel, in_specs=[SMEM, HBM] + [VMEM] * 2 + [HBM] *...  3.34 us
    pallas_call x1, Pallas kernels, body(): pl.pallas_call(outbox_kernel, in_specs=[SMEM] + [HBM] * 4, out_specs=VMEM...  3.06 us
  transfers between devices with their start and end apart: 11, of which 5 were waited for; matrix products, arithmetic and copies ran while one was open for 0% of the time, Pallas kernels for 4%

profile of v5, /device:TPU:8, one launch (start us, length us, event | category | flops | bytes accessed | tf_op | source)
XLA Modules:
  0.0 140.5 jit_solution(2546788918852789874)
XLA Ops:
  0.6 0.1 pad_add_fusion.at_ref
  0.7 3.1 %shard_map.86 = bf16[8,4,8,3072]{3,2,1,0:T(8,128)(2,1)} custom-call(s32[2]{0:T(128)S(1)} %pad_add_fusion.at_ref, bf16[16,3072]{1,0:T(8,128)(2,1)} %tokens_hbm.1, bf16[16,3072]{1,0:T(8,128)(2,1)} %cot_hbm.1, s32[2,16]{1,0:T(2,128)} %bitcast.13, f32[2,16]{1,0:T(2,128)} %bitcast.12), custom_call_target="tpu_custom_call" | custom-call | tf_op jit(solution)/shard_map/pallas_call | solution.py:219
  3.8 13.3 %all-to-all-start = ((bf16[32,8,3072]{2,1,0:T(8,128)(2,1)}), bf16[32,8,3072]{2,1,0:T(8,128)(2,1)}, u32[]{:S(2)}, u32[]{:S(2)}) async-start(bf16[32,8,3072]{2,1,0:T(8,128)(2,1)} %bitcast.4), calls=%async_computation | async-start | bytes 3145728 | tf_op jit(solution)/shard_map/all_to_all | solution.py:227
  17.1 2.6 %shard_map.87 = (bf16[192,512]{1,0:T(8,128)(2,1)S(1)}, bf16[192,512]{1,0:T(8,128)(2,1)S(1)}, bf16[192,512]{1,0:T(8,128)(2,1)S(1)}, bf16[192,512]{1,0:T(8,128)(2,...) custom-call(s32[2]{0:T(128)S(1)} %pad_add_fusion.at_ref, ...), custom_call_target="tpu_custom_call" | custom-call | tf_op jit(solution)/shard_map/pallas_call | solution.py:229
  19.7 1.9 %collective-permute-start = (bf16[2,1536,256]{2,1,0:T(8,128)(2,1)S(1)}, bf16[2,1536,256]{2,1,0:T(8,128)(2,1)S(1)}, u32[]{:S(2)}, u32[]{:S(2)}) collective-permute-start(bf16[2,1536,256]{2,1,0:T(8,128)(2,1)S(1)} %get-tuple-element.31), channel_id=1, source_target_pairs={{0,1},{1,0},{2,3},{3,2},{4,5},{5,4},{6,7},{7,6},{8,9},{9,8},{10,11... | collective-permute-start | bytes 4718600 | tf_op jit(solution)/shard_map/ppermute | solution.py:237
  21.7 6.8 %collective-permute-start.1 = (bf16[192,512]{1,0:T(8,128)(2,1)S(1)}, bf16[192,512]{1,0:T(8,128)(2,1)S(1)}, u32[]{:S(2)}, u32[]{:S(2)}) collective-permute-start(bf16[192,512]{1,0:T(8,128)(2,1)S(1)} %get-tuple-element.35), channel_id=1, source_target_pairs={{0,8},{2,10},{4,12},{6,14},{8,0},{10,2},{12,4},{14,6},{1,9},{3,11}... | collective-permute-start | bytes 589832 | tf_op jit(solution)/shard_map/ppermute | solution.py:240
  28.5 1.9 %collective-permute-start.2 = (bf16[192,512]{1,0:T(8,128)(2,1)S(1)}, bf16[192,512]{1,0:T(8,128)(2,1)S(1)}, u32[]{:S(2)}, u32[]{:S(2)}) collective-permute-start(bf16[192,512]{1,0:T(8,128)(2,1)S(1)} %get-tuple-element.36), channel_id=1, source_target_pairs={{0,6},{2,8},{4,10},{6,12},{8,14},{10,0},{12,2},{14,4},{1,7},{3,9},... | collective-permute-start | bytes 589832 | tf_op jit(solution)/shard_map/ppermute | solution.py:240
  30.4 6.9 %collective-permute-start.3 = (bf16[192,512]{1,0:T(8,128)(2,1)S(1)}, bf16[192,512]{1,0:T(8,128)(2,1)S(1)}, u32[]{:S(2)}, u32[]{:S(2)}) collective-permute-start(bf16[192,512]{1,0:T(8,128)(2,1)S(1)} %get-tuple-element.37), channel_id=1, source_target_pairs={{0,10},{2,12},{4,14},{6,0},{8,2},{10,4},{12,6},{14,8},{1,11},{3,13... | collective-permute-start | bytes 589832 | tf_op jit(solution)/shard_map/ppermute | solution.py:240
  37.4 1.9 %collective-permute-start.4 = (bf16[192,512]{1,0:T(8,128)(2,1)S(1)}, bf16[192,512]{1,0:T(8,128)(2,1)S(1)}, u32[]{:S(2)}, u32[]{:S(2)}) collective-permute-start(bf16[192,512]{1,0:T(8,128)(2,1)S(1)} %get-tuple-element.38), channel_id=1, source_target_pairs={{0,4},{2,6},{4,8},{6,10},{8,12},{10,14},{12,0},{14,2},{1,5},{3,7},... | collective-permute-start | bytes 589832 | tf_op jit(solution)/shard_map/ppermute | solution.py:240
  39.3 6.0 %collective-permute-start.5 = (bf16[192,512]{1,0:T(8,128)(2,1)S(1)}, bf16[192,512]{1,0:T(8,128)(2,1)S(1)}, u32[]{:S(2)}, u32[]{:S(2)}) collective-permute-start(bf16[192,512]{1,0:T(8,128)(2,1)S(1)} %get-tuple-element.39), channel_id=1, source_target_pairs={{0,12},{2,14},{4,0},{6,2},{8,4},{10,6},{12,8},{14,10},{1,13},{3,15... | collective-permute-start | bytes 589832 | tf_op jit(solution)/shard_map/ppermute | solution.py:240
  45.4 1.9 %collective-permute-start.6 = (bf16[192,512]{1,0:T(8,128)(2,1)S(1)}, bf16[192,512]{1,0:T(8,128)(2,1)S(1)}, u32[]{:S(2)}, u32[]{:S(2)}) collective-permute-start(bf16[192,512]{1,0:T(8,128)(2,1)S(1)} %get-tuple-element.40), channel_id=1, source_target_pairs={{0,2},{2,4},{4,6},{6,8},{8,10},{10,12},{12,14},{14,0},{1,3},{3,5},... | collective-permute-start | bytes 589832 | tf_op jit(solution)/shard_map/ppermute | solution.py:240
  47.3 4.5 %collective-permute-done.2.rest_1_ = bf16[192,512]{1,0:T(8,128)(2,1)S(1)} collective-permute-done((bf16[192,512]{1,0:T(8,128)(2,1)S(1)}, bf16[192,512]{1,0:T(8,128)(2,1)S(1)}, u32[]{:S(2)}, u32[]{:S(2)}) %collective-permute-start.2) | collective-permute-done | bytes 196640 | tf_op jit(solution)/shard_map/ppermute | solution.py:240
  51.8 1.9 %collective-permute-start.7 = (bf16[192,512]{1,0:T(8,128)(2,1)S(1)}, bf16[192,512]{1,0:T(8,128)(2,1)}, u32[]{:S(2)}, u32[]{:S(2)}) collective-permute-start(bf16[192,512]{1,0:T(8,128)(2,1)S(1)} %get-tuple-element.41), channel_id=1, source_target_pairs={{0,14},{2,0},{4,2},{6,4},{8,6},{10,8},{12,10},{14,12},{1,15},{3,1}... | collective-permute-start | bytes 589832 | tf_op jit(solution)/shard_map/ppermute | solution.py:240
  53.7 2.3 %shard_map.88 = (bf16[8,192,512]{2,1,0:T(8,128)(2,1)S(1)}, bf16[8,192,512]{2,1,0:T(8,128)(2,1)S(1)}) custom-call(s32[2]{0:T(128)S(1)} %pad_add_fusion.at_ref, bf16[3072,256]{1,0:T(8,128)(2,1)} %gate_hbm.3, bf16[3072,256]{1,0:T(8,128)(2,1)} %up_hbm.3, bf16[2,1536,256]{2,1,0:T(8,128)(2,1)S(1)} %collective-permute-done.far_hbm), custom_call_target="tpu_custom_call" | custom-call | tf_op jit(solution)/shard_map/pallas_call | solution.py:242
  56.1 0.0 collective-permute-done.3.rest_2_
  56.1 4.1 %collective-permute-done.4.rest_3_ = bf16[192,512]{1,0:T(8,128)(2,1)S(1)} collective-permute-done((bf16[192,512]{1,0:T(8,128)(2,1)S(1)}, bf16[192,512]{1,0:T(8,128)(2,1)S(1)}, u32[]{:S(2)}, u32[]{:S(2)}) %collective-permute-start.4) | collective-permute-done | bytes 196640 | tf_op jit(solution)/shard_map/ppermute | solution.py:240
  60.2 0.0 collective-permute-done.5.rest_4_
  60.2 4.4 %collective-permute-done.6.rest_5_ = bf16[192,512]{1,0:T(8,128)(2,1)S(1)} collective-permute-done((bf16[192,512]{1,0:T(8,128)(2,1)S(1)}, bf16[192,512]{1,0:T(8,128)(2,1)S(1)}, u32[]{:S(2)}, u32[]{:S(2)}) %collective-permute-start.6) | collective-permute-done | bytes 196640 | tf_op jit(solution)/shard_map/ppermute | solution.py:240
  64.7 0.7 copy-done.5
  65.3 3.3 %shard_map.89 = (f32[3,256,512]{2,1,0:T(8,128)S(1)}, bf16[8,192,512]{2,1,0:T(8,128)(2,1)S(1)}) custom-call(s32[2]{0:T(128)S(1)} %pad_add_fusion.at_ref, bf16[256,3072]{1,0:T(8,128)(2,1)} %bitcast.6.got_hbm, bf16[8,192,512]{2,1,0:T(8,128)(2,1)S(1)} %get-tuple-element.43.gate_w, bf16[8,192,512]{2,1,0:T(8,128)(2,1)S(1)} %get-tuple-element.44.up_w, ...), custom_call_target="tpu_custom_call" | custom-call | tf_op jit(solution)/shard_map/pallas_call | solution.py:251
  68.7 1.9 %collective-permute-start.8 = (f32[3,256,512]{2,1,0:T(8,128)S(1)}, f32[3,256,512]{2,1,0:T(8,128)S(1)}, u32[]{:S(2)}, u32[]{:S(2)}) collective-permute-start(f32[3,256,512]{2,1,0:T(8,128)S(1)} %get-tuple-element.52.part_ref), channel_id=1, source_target_pairs={{0,1},{1,0},{2,3},{3,2},{4,5},{5,4},{6,7},{7,6},{8,9},{9,8},{10,11... | collective-permute-start | bytes 4718600 | tf_op jit(solution)/shard_map/ppermute | solution.py:267
  70.6 3.4 %collective-permute-done.8.came_ref = f32[3,256,512]{2,1,0:T(8,128)S(1)} collective-permute-done((f32[3,256,512]{2,1,0:T(8,128)S(1)}, f32[3,256,512]{2,1,0:T(8,128)S(1)}, u32[]{:S(2)}, u32[]{:S(2)}) %collective-permute-start.8) | collective-permute-done | bytes 1572896 | tf_op jit(solution)/shard_map/ppermute | solution.py:267
  74.0 3.0 %shard_map.90 = bf16[256,3072]{1,0:T(8,128)(2,1)} custom-call(s32[2]{0:T(128)S(1)} %pad_add_fusion.at_ref, f32[3,256,512]{2,1,0:T(8,128)S(1)} %get-tuple-element.52.part_ref, f32[3,256,512]{2,1,0:T(8,128)S(1)} %collective-permute-done.8.came_ref, bf16[8,192,512]{2,1,0:T(8,128)(2,1)S(1)} %get-tuple-element.43.gate_w, ...), custom_call_target="tpu_custom_call" | custom-call | tf_op jit(solution)/shard_map/pallas_call | solution.py:260
  77.0 0.0 copy-start.6
  77.0 0.0 copy-start.7
  77.0 9.7 %all-to-all-start.1 = ((bf16[32,8,3072]{2,1,0:T(8,128)(2,1)}), bf16[32,8,3072]{2,1,0:T(8,128)(2,1)S(1)}, u32[]{:S(2)}, u32[]{:S(2)}) async-start(bf16[32,8,3072]{2,1,0:T(8,128)(2,1)} %bitcast.7), calls=%async_computation.1 | async-start | bytes 3145728 | tf_op jit(solution)/shard_map/all_to_all | solution.py:268
  86.8 0.1 copy.10.gates_ref
  86.9 0.1 copy.9.routes_ref
  87.0 39.4 %all-to-all-done.1 = bf16[32,8,3072]{2,1,0:T(8,128)(2,1)S(1)} async-done(((bf16[32,8,3072]{2,1,0:T(8,128)(2,1)}), bf16[32,8,3072]{2,1,0:T(8,128)(2,1)S(1)}, u32[]{:S(2)}, u32[]{:S(2)}) %all-to-all-start.1) | async-done | bytes 1572896 | tf_op jit(solution)/shard_map/all_to_all | solution.py:268
  126.4 0.7 shard_map.91
  127.1 12.7 %all_to_all.15 = bf16[8,16,384]{2,1,0:T(8,128)(2,1)S(1)} all-to-all(bf16[8,16,384]{2,1,0:T(8,128)(2,1)S(1)} %shard_map.91), channel_id=1, replica_groups=mesh['x'=4,'z'=8,'y'=8,'c'=2] {'y'}, dimensions={0} | all-to-all | bytes 196608 | tf_op jit(solution)/shard_map/all_to_all | solution.py:274
  139.8 0.7 fusion
  (18 shorter events, 0.1 us)
Async XLA Ops:
  3.8 61.6 %all-to-all-start = ((bf16[32,8,3072]{2,1,0:T(8,128)(2,1)}), bf16[32,8,3072]{2,1,0:T(8,128)(2,1)}, u32[]{:S(2)}, u32[]{:S(2)}) async-start(bf16[32,8,3072]{2,1,0:T(8,128)(2,1)} %bitcast.4), calls=%async_computation | async-start | bytes 3145728 | tf_op jit(solution)/shard_map/all_to_all | solution.py:227
  19.7 19.6 %collective-permute-start = (bf16[2,1536,256]{2,1,0:T(8,128)(2,1)S(1)}, bf16[2,1536,256]{2,1,0:T(8,128)(2,1)S(1)}, u32[]{:S(2)}, u32[]{:S(2)}) collective-permute-start(bf16[2,1536,256]{2,1,0:T(8,128)(2,1)S(1)} %get-tuple-element.31), channel_id=1, source_target_pairs={{0,1},{1,0},{2,3},{3,2},{4,5},{5,4},{6,7},{7,6},{8,9},{9,8},{10,11... | collective-permute-start | bytes 4718600 | tf_op jit(solution)/shard_map/ppermute | solution.py:237
  21.7 23.7 %collective-permute-start.1 = (bf16[192,512]{1,0:T(8,128)(2,1)S(1)}, bf16[192,512]{1,0:T(8,128)(2,1)S(1)}, u32[]{:S(2)}, u32[]{:S(2)}) collective-permute-start(bf16[192,512]{1,0:T(8,128)(2,1)S(1)} %get-tuple-element.35), channel_id=1, source_target_pairs={{0,8},{2,10},{4,12},{6,14},{8,0},{10,2},{12,4},{14,6},{1,9},{3,11}... | collective-permute-start | bytes 589832 | tf_op jit(solution)/shard_map/ppermute | solution.py:240
  28.5 23.3 %collective-permute-start.2 = (bf16[192,512]{1,0:T(8,128)(2,1)S(1)}, bf16[192,512]{1,0:T(8,128)(2,1)S(1)}, u32[]{:S(2)}, u32[]{:S(2)}) collective-permute-start(bf16[192,512]{1,0:T(8,128)(2,1)S(1)} %get-tuple-element.36), channel_id=1, source_target_pairs={{0,6},{2,8},{4,10},{6,12},{8,14},{10,0},{12,2},{14,4},{1,7},{3,9},... | collective-permute-start | bytes 589832 | tf_op jit(solution)/shard_map/ppermute | solution.py:240
  30.4 25.7 %collective-permute-start.3 = (bf16[192,512]{1,0:T(8,128)(2,1)S(1)}, bf16[192,512]{1,0:T(8,128)(2,1)S(1)}, u32[]{:S(2)}, u32[]{:S(2)}) collective-permute-start(bf16[192,512]{1,0:T(8,128)(2,1)S(1)} %get-tuple-element.37), channel_id=1, source_target_pairs={{0,10},{2,12},{4,14},{6,0},{8,2},{10,4},{12,6},{14,8},{1,11},{3,13... | collective-permute-start | bytes 589832 | tf_op jit(solution)/shard_map/ppermute | solution.py:240
  37.4 22.8 %collective-permute-start.4 = (bf16[192,512]{1,0:T(8,128)(2,1)S(1)}, bf16[192,512]{1,0:T(8,128)(2,1)S(1)}, u32[]{:S(2)}, u32[]{:S(2)}) collective-permute-start(bf16[192,512]{1,0:T(8,128)(2,1)S(1)} %get-tuple-element.38), channel_id=1, source_target_pairs={{0,4},{2,6},{4,8},{6,10},{8,12},{10,14},{12,0},{14,2},{1,5},{3,7},... | collective-permute-start | bytes 589832 | tf_op jit(solution)/shard_map/ppermute | solution.py:240
  39.3 20.9 %collective-permute-start.5 = (bf16[192,512]{1,0:T(8,128)(2,1)S(1)}, bf16[192,512]{1,0:T(8,128)(2,1)S(1)}, u32[]{:S(2)}, u32[]{:S(2)}) collective-permute-start(bf16[192,512]{1,0:T(8,128)(2,1)S(1)} %get-tuple-element.39), channel_id=1, source_target_pairs={{0,12},{2,14},{4,0},{6,2},{8,4},{10,6},{12,8},{14,10},{1,13},{3,15... | collective-permute-start | bytes 589832 | tf_op jit(solution)/shard_map/ppermute | solution.py:240
  45.4 10.7 %copy-start = (bf16[192,512]{1,0:T(8,128)(2,1)}, bf16[192,512]{1,0:T(8,128)(2,1)S(1)}, u32[]{:S(2)}) copy-start(bf16[192,512]{1,0:T(8,128)(2,1)S(1)} %collective-permute-done.1.rest_0_) | copy-start | bytes 589828
  45.4 19.3 %collective-permute-start.6 = (bf16[192,512]{1,0:T(8,128)(2,1)S(1)}, bf16[192,512]{1,0:T(8,128)(2,1)S(1)}, u32[]{:S(2)}, u32[]{:S(2)}) collective-permute-start(bf16[192,512]{1,0:T(8,128)(2,1)S(1)} %get-tuple-element.40), channel_id=1, source_target_pairs={{0,2},{2,4},{4,6},{6,8},{8,10},{10,12},{12,14},{14,0},{1,3},{3,5},... | collective-permute-start | bytes 589832 | tf_op jit(solution)/shard_map/ppermute | solution.py:240
  51.8 4.3 %copy-start.1 = (bf16[192,512]{1,0:T(8,128)(2,1)}, bf16[192,512]{1,0:T(8,128)(2,1)S(1)}, u32[]{:S(2)}) copy-start(bf16[192,512]{1,0:T(8,128)(2,1)S(1)} %collective-permute-done.2.rest_1_) | copy-start | bytes 589828
  51.8 13.5 %collective-permute-start.7 = (bf16[192,512]{1,0:T(8,128)(2,1)S(1)}, bf16[192,512]{1,0:T(8,128)(2,1)}, u32[]{:S(2)}, u32[]{:S(2)}) collective-permute-start(bf16[192,512]{1,0:T(8,128)(2,1)S(1)} %get-tuple-element.41), channel_id=1, source_target_pairs={{0,14},{2,0},{4,2},{6,4},{8,6},{10,8},{12,10},{14,12},{1,15},{3,1}... | collective-permute-start | bytes 589832 | tf_op jit(solution)/shard_map/ppermute | solution.py:240
  56.1 8.6 %copy-start.2 = (bf16[192,512]{1,0:T(8,128)(2,1)}, bf16[192,512]{1,0:T(8,128)(2,1)S(1)}, u32[]{:S(2)}) copy-start(bf16[192,512]{1,0:T(8,128)(2,1)S(1)} %collective-permute-done.3.rest_2_) | copy-start | bytes 589828
  60.2 4.5 %copy-start.3 = (bf16[192,512]{1,0:T(8,128)(2,1)}, bf16[192,512]{1,0:T(8,128)(2,1)S(1)}, u32[]{:S(2)}) copy-start(bf16[192,512]{1,0:T(8,128)(2,1)S(1)} %collective-permute-done.4.rest_3_) | copy-start | bytes 589828
  60.2 4.5 %copy-start.4 = (bf16[192,512]{1,0:T(8,128)(2,1)}, bf16[192,512]{1,0:T(8,128)(2,1)S(1)}, u32[]{:S(2)}) copy-start(bf16[192,512]{1,0:T(8,128)(2,1)S(1)} %collective-permute-done.5.rest_4_) | copy-start | bytes 589828
  64.6 0.7 copy-start.5
  68.7 5.3 %collective-permute-start.8 = (f32[3,256,512]{2,1,0:T(8,128)S(1)}, f32[3,256,512]{2,1,0:T(8,128)S(1)}, u32[]{:S(2)}, u32[]{:S(2)}) collective-permute-start(f32[3,256,512]{2,1,0:T(8,128)S(1)} %get-tuple-element.52.part_ref), channel_id=1, source_target_pairs={{0,1},{1,0},{2,3},{3,2},{4,5},{5,4},{6,7},{7,6},{8,9},{9,8},{10,11... | collective-permute-start | bytes 4718600 | tf_op jit(solution)/shard_map/ppermute | solution.py:267
  77.0 9.8 %copy-start.6 = (f32[16,2]{0,1:T(2,128)S(1)}, f32[16,2]{0,1:T(2,128)}, u32[]{:S(2)}) copy-start(f32[16,2]{0,1:T(2,128)} %param.10) | copy-start | bytes 388
  77.0 9.9 %copy-start.7 = (s32[16,2]{0,1:T(2,128)S(1)}, s32[16,2]{0,1:T(2,128)}, u32[]{:S(2)}) copy-start(s32[16,2]{0,1:T(2,128)} %param.9) | copy-start | bytes 388
  77.0 49.3 %all-to-all-start.1 = ((bf16[32,8,3072]{2,1,0:T(8,128)(2,1)}), bf16[32,8,3072]{2,1,0:T(8,128)(2,1)S(1)}, u32[]{:S(2)}, u32[]{:S(2)}) async-start(bf16[32,8,3072]{2,1,0:T(8,128)(2,1)} %bitcast.7), calls=%async_computation.1 | async-start | bytes 3145728 | tf_op jit(solution)/shard_map/all_to_all | solution.py:268
